TPU v7x, 256 devices: a whole 4x4x8 slice. The times are simulated.
256 devices in a mesh: pool: 64 (over z, x, core), rep: 4 (over y).
Axes of the slice: x: 4, y: 4, z: 8, core: 2. Of those that a mesh axis runs over, the one named last changes fastest.
Arguments:
- query_vecs: bfloat16 [4096, 32, 128], P(('pool', 'rep')), may hold values from -0.5 to 0.5
- passage_vecs: bfloat16 [2048, 256, 128], P('pool'), may hold values from -0.5 to 0.5
- owner_ids: int32 [4096, 4], P(('pool', 'rep')), may hold values from 0 to 63, all different within a row; in each aligned block of 16 rows (0 to 15, 16 to 31, ...) at most 2 rows name the same one
- local_ids: int32 [4096, 4, 4], P(('pool', 'rep')), may hold values from 0 to 31
- cand_mask: int32 [4096, 16], P(('pool', 'rep')), may hold values 0 or 1
Outputs:
- query_loss: float32 [4096], P(('pool', 'rep'))
- grad_query: float32 [4096, 32, 128], P(('pool', 'rep'))
- grad_passage: float32 [2048, 256, 128], P('pool', 'rep')
Inputs may be any that keep to these rules, and one draw needn't show every extreme that they name: `owner_ids`: each row names 4 different pool shards. Among the 16 rows of one device no shard is named more than 2 times, and in some devices' rows one shard is named exactly 2 times.
All inputs are finite; a program needn't handle non-finite values. No bound on the sum of `cand_mask` on one device may be relied on, other than what follows from the above.
Results may differ from a plain program's by a relative error of at most 0.014.
Values may be sent and summed in bfloat16 or wider, within the bound.
A program may use at most 128 MiB of HBM per device.

v0:
```python
import jax
import jax.numpy as jnp
from jax import lax
from jax.sharding import PartitionSpec as P

temper = 0.05
loss_scale = 16.0
epsilon = 1e-06


def normalize(vectors):
    widened = vectors.astype(jnp.float32)
    inverse = lax.rsqrt(jnp.sum(widened * widened, axis=-1, keepdims=True) + epsilon)
    return (widened * inverse, inverse)


def unit_backward(unit_vecs, inverse, upstream):
    return inverse * (upstream - unit_vecs * jnp.sum(unit_vecs * upstream, axis=-1, keepdims=True))


def candidate_loss(scores, valid_flags):
    exp_terms = jnp.exp(scores) * valid_flags.astype(jnp.float32)
    denominator = jnp.sum(exp_terms, axis=-1, keepdims=True)
    denominator = jnp.where(denominator > 0.0, denominator, 1.0)
    is_first = (jnp.arange(scores.shape[-1]) == 0).astype(jnp.float32)
    losses = jnp.log(denominator[:, 0]) - scores[:, 0]
    return (losses, loss_scale * (exp_terms / denominator - is_first))


def block_size(row_total, upper_bound):
    chosen = 1
    for divisor in range(1, upper_bound + 1):
        if row_total % divisor == 0:
            chosen = divisor
    return chosen


def soft_weights(sim_scores, log_sums, weights):
    return (weights[:, :, None, None] * jnp.exp(sim_scores / temper - log_sums[..., None])).astype(
        jnp.bfloat16
    )


def one_hot_rows(cand_rows, table_rows, dtype):
    table_ids = jnp.arange(table_rows, dtype=jnp.int32)
    return (cand_rows[..., None] == table_ids).astype(dtype)


def pick_rows(table, cand_rows):
    selector = one_hot_rows(cand_rows, table.shape[0], jnp.bfloat16)
    return jnp.einsum("bjp,pkd->bjkd", selector, table, preferred_element_type=jnp.float32).astype(
        jnp.bfloat16
    )


def add_rows(accumulated, cand_rows, passage_grad):
    selector = one_hot_rows(cand_rows, accumulated.shape[0], jnp.float32)
    return accumulated + jnp.einsum(
        "bjp,bjkd->pkd", selector, passage_grad, precision=lax.Precision.HIGHEST
    )


def per_device(query_vecs, passage_vecs, owner_ids, local_ids, cand_mask):
    query_rows, query_len, feature_dim = query_vecs.shape
    passage_rows, passage_len, _ = passage_vecs.shape
    group_count = owner_ids.shape[1]
    group_width = local_ids.shape[2]
    cand_total = group_count * group_width
    pool_size = lax.axis_size("pool")
    capacity = (query_rows * group_count + pool_size - 1) // pool_size + 1
    slot_total = pool_size * capacity
    pair_total = query_rows * group_count
    q_unit, q_inverse = normalize(query_vecs)
    q_low = q_unit.astype(jnp.bfloat16)
    p_unit, p_inverse = normalize(passage_vecs)
    p_low = p_unit.astype(jnp.bfloat16)
    flat_owner = owner_ids.reshape(pair_total)
    pair_ids = jnp.arange(pair_total, dtype=jnp.int32)
    earlier = pair_ids[None, :] // group_count < pair_ids[:, None] // group_count
    same_owner = flat_owner[None, :] == flat_owner[:, None]
    slot_rank = jnp.sum((earlier & same_owner).astype(jnp.int32), axis=1)
    slot_of_pair = flat_owner * capacity + slot_rank
    slot_ids = jnp.arange(slot_total, dtype=jnp.int32)
    slot_match = slot_of_pair[None, :] == slot_ids[:, None]
    filled = jnp.any(slot_match, axis=1)
    pair_of_slot = jnp.sum(jnp.where(slot_match, pair_ids[None, :], 0), axis=1)
    row_match = jnp.any(slot_match.reshape(slot_total, query_rows, group_count), axis=2).astype(
        jnp.bfloat16
    )
    is_first = (jnp.arange(cand_total) == 0).astype(jnp.int32)
    valid_flags = jnp.maximum(cand_mask, is_first[None, :])
    local_pairs = local_ids.reshape(pair_total, group_width)
    valid_pairs = valid_flags.reshape(pair_total, group_width)
    filled_int = filled.astype(jnp.int32)[:, None]
    q_slots = jnp.dot(
        row_match,
        q_low.reshape(query_rows, query_len * feature_dim),
        preferred_element_type=jnp.float32,
    ).astype(jnp.bfloat16)
    meta_rows = local_pairs[pair_of_slot] * filled_int
    meta = jnp.concatenate([meta_rows, valid_pairs[pair_of_slot] * filled_int], axis=1)
    recv_q, recv_meta = (
        lax.all_to_all(
            q_slots.reshape(pool_size, capacity, query_len, feature_dim),
            "pool",
            split_axis=0,
            concat_axis=0,
            tiled=True,
        ),
        lax.all_to_all(
            meta.reshape(pool_size, capacity, meta.shape[1]),
            "pool",
            split_axis=0,
            concat_axis=0,
            tiled=True,
        ),
    )
    recv_q = recv_q.reshape(slot_total, query_len, feature_dim)
    recv_meta = recv_meta.reshape(slot_total, meta.shape[1])
    recv_rows = recv_meta[:, :group_width]
    block_rows = block_size(slot_total, 16)
    block_count = slot_total // block_rows

    def forward_block(block_input):
        queries, cand_rows = block_input
        candidates = pick_rows(p_low, cand_rows)
        sim_scores = jnp.einsum(
            "bid,bjkd->bjik", queries, candidates, preferred_element_type=jnp.float32
        )
        log_sums = jnp.log(jnp.sum(jnp.exp(sim_scores / temper), axis=-1))
        return (temper * jnp.sum(log_sums, axis=-1), log_sums)

    scores_local, log_local = lax.map(
        forward_block,
        (
            recv_q.reshape(block_count, block_rows, query_len, feature_dim),
            recv_rows.reshape(block_count, block_rows, group_width),
        ),
    )
    scores_local = scores_local.reshape(slot_total, group_width)
    log_local = log_local.reshape(slot_total, group_width, query_len)
    returned_scores = lax.all_to_all(
        scores_local.reshape(pool_size, capacity, group_width),
        "pool",
        split_axis=0,
        concat_axis=0,
        tiled=True,
    ).reshape(slot_total, group_width)
    pair_scores = returned_scores[slot_of_pair].reshape(query_rows, cand_total)
    losses, dscore = candidate_loss(pair_scores, valid_flags)
    dpair = dscore.reshape(pair_total, group_width)
    dslot = jnp.where(filled[:, None], dpair[pair_of_slot], 0.0)
    weights = lax.all_to_all(
        dslot.reshape(pool_size, capacity, group_width),
        "pool",
        split_axis=0,
        concat_axis=0,
        tiled=True,
    ).reshape(slot_total, group_width)

    def both_block(accumulated, block_input):
        queries, cand_rows, log_sums, block_weights = block_input
        candidates = pick_rows(p_low, cand_rows)
        sim_scores = jnp.einsum(
            "bid,bjkd->bjik", queries, candidates, preferred_element_type=jnp.float32
        )
        dsoft = soft_weights(sim_scores, log_sums, block_weights)
        query_grad = jnp.einsum(
            "bjik,bjkd->bid", dsoft, candidates, preferred_element_type=jnp.float32
        ).astype(jnp.bfloat16)
        passage_grad = jnp.einsum(
            "bjik,bid->bjkd", dsoft, queries, preferred_element_type=jnp.float32
        )
        return (add_rows(accumulated, cand_rows, passage_grad), query_grad)

    block_inputs = (
        recv_q.reshape(block_count, block_rows, query_len, feature_dim),
        recv_rows.reshape(block_count, block_rows, group_width),
        log_local.reshape(block_count, block_rows, group_width, query_len),
        weights.reshape(block_count, block_rows, group_width),
    )
    rep_size = lax.axis_size("rep")
    token_share = passage_len // rep_size
    token_start = lax.axis_index("rep") * token_share
    start_grad = jnp.zeros((passage_rows, passage_len, feature_dim), jnp.float32)
    passage_total, query_slots = lax.scan(both_block, start_grad, block_inputs)
    share_sum = lax.psum_scatter(
        passage_total.astype(jnp.bfloat16), "rep", scatter_dimension=1, tiled=True
    ).astype(jnp.float32)
    query_slots = query_slots.reshape(slot_total, query_len, feature_dim)
    returned = lax.all_to_all(
        query_slots.reshape(pool_size, capacity, query_len, feature_dim),
        "pool",
        split_axis=0,
        concat_axis=0,
        tiled=True,
    ).reshape(slot_total, query_len * feature_dim)
    g_query = jnp.einsum(
        "sq,sx->qx", row_match, returned, preferred_element_type=jnp.float32
    ).reshape(query_rows, query_len, feature_dim)
    grad_query = unit_backward(q_unit, q_inverse, g_query)
    unit_share = lax.dynamic_slice_in_dim(p_unit, token_start, token_share, 1)
    inverse_share = lax.dynamic_slice_in_dim(p_inverse, token_start, token_share, 1)
    grad_passage = unit_backward(unit_share, inverse_share, share_sum)
    return (losses, grad_query, grad_passage)


def solution(mesh):
    return jax.shard_map(
        per_device,
        mesh=mesh,
        in_specs=(
            P(("pool", "rep"), None, None),
            P("pool", None, None),
            P(("pool", "rep"), None),
            P(("pool", "rep"), None, None),
            P(("pool", "rep"), None),
        ),
        out_specs=(P(("pool", "rep")), P(("pool", "rep"), None, None), P("pool", "rep", None)),
        check_vma=False,
    )
```

profile of v0, /device:TPU:1, one launch (start us, length us, event | category | flops | bytes accessed | tf_op | source)
XLA Modules:
  0.0 381.9 jit_solution(8314877929534315692)
XLA Ops:
  13.1 13.0 %all-to-all-start = ((s32[64,2,8]{2,1,0:T(2,128)}), s32[64,2,8]{2,1,0:T(2,128)S(1)}, u32[]{:S(2)}, u32[]{:S(2)}) async-start(s32[64,2,8]{2,1,0:T(2,128)} %copy.145), calls=%async_computation | async-start | bytes 131072 | tf_op jit(solution)/shard_map/all_to_all | solution.py:110
  30.1 6.1 %all-to-all-done = s32[64,2,8]{2,1,0:T(2,128)S(1)} async-done(((s32[64,2,8]{2,1,0:T(2,128)}), s32[64,2,8]{2,1,0:T(2,128)S(1)}, u32[]{:S(2)}, u32[]{:S(2)}) %all-to-all-start) | async-done | bytes 4128 | tf_op jit(solution)/shard_map/all_to_all | solution.py:110
  36.2 4.5 %all-to-all-start.1 = ((bf16[64,2,32,128]{3,2,1,0:T(8,128)(2,1)}), bf16[64,2,32,128]{3,2,1,0:T(8,128)(2,1)S(1)}, u32[]{:S(2)}, u32[]{:S(2)}) async-start(bf16[64,2,32,128]{3,2,1,0:T(8,128)(2,1)} %bitcast.50), calls=%async_computation.1 | async-start | bytes 2097152 | tf_op jit(solution)/shard_map/all_to_all | solution.py:103
  42.0 3.1 convert_multiply_fusion
  47.2 21.7 %all-to-all-done.1 = bf16[64,2,32,128]{3,2,1,0:T(8,128)(2,1)S(1)} async-done(((bf16[64,2,32,128]{3,2,1,0:T(8,128)(2,1)}), bf16[64,2,32,128]{3,2,1,0:T(8,128)(2,1)S(1)}, u32[]{:S(2)}, u32[]{:S(2)}) %all-to-all-start.1) | async-done | bytes 1048608 | tf_op jit(solution)/shard_map/all_to_all | solution.py:103
  68.9 38.7 %while.25 = (s32[]{:T(128)}, f32[8,16,4]{1,2,0:T(4,128)S(1)}, f32[8,16,4,32]{3,2,1,0:T(4,128)S(1)}, s32[8,16,4]{1,2,0:T(4,128)}, bf16[32,256,128]{2,0,1:T(8,128)...) while((s32[]{:T(128)}, f32[8,16,4]{1,2,0:T(4,128)S(1)}, f32[8,16,4,32]{3,2,1,0:T(4,128)S(1)}, ...), condition=%wide.region_9.10_spmd, body=%wide.region_6.9_spmd.sunk | while | flops 271583232 | bytes 10704997 | solution.py:133
  108.3 6.4 %all-to-all-start.2 = ((f32[64,2,4]{2,1,0:T(2,128)}), f32[64,2,4]{2,1,0:T(2,128)S(1)}, u32[]{:S(2)}, u32[]{:S(2)}) async-start(f32[64,2,4]{2,1,0:T(2,128)} %bitcast.17), calls=%async_computation.2 | async-start | bytes 131072 | tf_op jit(solution)/shard_map/all_to_all | solution.py:142
  115.3 9.5 %all-to-all-done.2 = f32[64,2,4]{2,1,0:T(2,128)S(1)} async-done(((f32[64,2,4]{2,1,0:T(2,128)}), f32[64,2,4]{2,1,0:T(2,128)S(1)}, u32[]{:S(2)}, u32[]{:S(2)}) %all-to-all-start.2) | async-done | bytes 2080 | tf_op jit(solution)/shard_map/all_to_all | solution.py:142
  130.2 4.4 %all-to-all-start.3 = ((f32[64,2,4]{2,1,0:T(2,128)}), f32[64,2,4]{2,1,0:T(2,128)S(1)}, u32[]{:S(2)}, u32[]{:S(2)}) async-start(f32[64,2,4]{2,1,0:T(2,128)} %broadcast_select_fusion), calls=%async_computation.3 | async-start | bytes 131072 | tf_op jit(solution)/shard_map/all_to_all | solution.py:153
  134.7 10.1 %all-to-all-done.3 = f32[64,2,4]{2,1,0:T(2,128)S(1)} async-done(((f32[64,2,4]{2,1,0:T(2,128)}), f32[64,2,4]{2,1,0:T(2,128)S(1)}, u32[]{:S(2)}, u32[]{:S(2)}) %all-to-all-start.3) | async-done | bytes 2080 | tf_op jit(solution)/shard_map/all_to_all | solution.py:153
  144.9 177.6 %while.26 = (s32[]{:T(128)}, f32[32,256,128]{2,0,1:T(8,128)}, bf16[8,16,32,128]{3,2,1,0:T(8,128)(2,1)}, s32[8,16,4]{1,2,0:T(4,128)}, f32[8,16,4]{1,2,0:T(4,128)S...) while((s32[]{:T(128)}, f32[32,256,128]{2,0,1:T(8,128)}, ...), condition=%wide.region_12.13_spmd.clone, body=%wide.region_11.12_spmd.clone.sunk | while | flops 1348538368 | bytes 76998856 | solution.py:186
  149.4 3.0 fusion.121
  154.5 10.7 %bitcast_add_fusion.3 = f32[32,256,128]{2,0,1:T(8,128)S(1)} fusion(f32[32,256,128]{2,0,1:T(8,128)S(1)} %copy-done, f32[16,4,256,128]{3,2,1,0:T(8,128)S(1)} %fusion.120, pred[]{:T(512)S(6)} %compare.15, s32[16,4]{0,1:T(4,128)S(1)} %dynamic-slice_bitcast_fusion.9), kind=kOutput, calls=%fused_computation.22.clone.1 | convolution fusion | flops 807405568 | bytes 16777472 | tf_op jit(solution)/shard_map/while/body/eval_jaxpr/bjp,bjkd->pkd/dot_general | solution.py:58
  171.6 3.0 fusion.121
  176.7 10.7 %bitcast_add_fusion.3 = f32[32,256,128]{2,0,1:T(8,128)S(1)} fusion(f32[32,256,128]{2,0,1:T(8,128)S(1)} %copy-done, f32[16,4,256,128]{3,2,1,0:T(8,128)S(1)} %fusion.120, pred[]{:T(512)S(6)} %compare.15, s32[16,4]{0,1:T(4,128)S(1)} %dynamic-slice_bitcast_fusion.9), kind=kOutput, calls=%fused_computation.22.clone.1 | convolution fusion | flops 807405568 | bytes 16777472 | tf_op jit(solution)/shard_map/while/body/eval_jaxpr/bjp,bjkd->pkd/dot_general | solution.py:58
  193.7 3.0 fusion.121
  198.9 10.7 %bitcast_add_fusion.3 = f32[32,256,128]{2,0,1:T(8,128)S(1)} fusion(f32[32,256,128]{2,0,1:T(8,128)S(1)} %copy-done, f32[16,4,256,128]{3,2,1,0:T(8,128)S(1)} %fusion.120, pred[]{:T(512)S(6)} %compare.15, s32[16,4]{0,1:T(4,128)S(1)} %dynamic-slice_bitcast_fusion.9), kind=kOutput, calls=%fused_computation.22.clone.1 | convolution fusion | flops 807405568 | bytes 16777472 | tf_op jit(solution)/shard_map/while/body/eval_jaxpr/bjp,bjkd->pkd/dot_general | solution.py:58
  215.9 3.0 fusion.121
  221.0 10.7 %bitcast_add_fusion.3 = f32[32,256,128]{2,0,1:T(8,128)S(1)} fusion(f32[32,256,128]{2,0,1:T(8,128)S(1)} %copy-done, f32[16,4,256,128]{3,2,1,0:T(8,128)S(1)} %fusion.120, pred[]{:T(512)S(6)} %compare.15, s32[16,4]{0,1:T(4,128)S(1)} %dynamic-slice_bitcast_fusion.9), kind=kOutput, calls=%fused_computation.22.clone.1 | convolution fusion | flops 807405568 | bytes 16777472 | tf_op jit(solution)/shard_map/while/body/eval_jaxpr/bjp,bjkd->pkd/dot_general | solution.py:58
  238.1 3.0 fusion.121
  243.2 10.7 %bitcast_add_fusion.3 = f32[32,256,128]{2,0,1:T(8,128)S(1)} fusion(f32[32,256,128]{2,0,1:T(8,128)S(1)} %copy-done, f32[16,4,256,128]{3,2,1,0:T(8,128)S(1)} %fusion.120, pred[]{:T(512)S(6)} %compare.15, s32[16,4]{0,1:T(4,128)S(1)} %dynamic-slice_bitcast_fusion.9), kind=kOutput, calls=%fused_computation.22.clone.1 | convolution fusion | flops 807405568 | bytes 16777472 | tf_op jit(solution)/shard_map/while/body/eval_jaxpr/bjp,bjkd->pkd/dot_general | solution.py:58
  260.3 3.0 fusion.121
  265.4 10.7 %bitcast_add_fusion.3 = f32[32,256,128]{2,0,1:T(8,128)S(1)} fusion(f32[32,256,128]{2,0,1:T(8,128)S(1)} %copy-done, f32[16,4,256,128]{3,2,1,0:T(8,128)S(1)} %fusion.120, pred[]{:T(512)S(6)} %compare.15, s32[16,4]{0,1:T(4,128)S(1)} %dynamic-slice_bitcast_fusion.9), kind=kOutput, calls=%fused_computation.22.clone.1 | convolution fusion | flops 807405568 | bytes 16777472 | tf_op jit(solution)/shard_map/while/body/eval_jaxpr/bjp,bjkd->pkd/dot_general | solution.py:58
  282.4 3.0 fusion.121
  287.6 10.7 %bitcast_add_fusion.3 = f32[32,256,128]{2,0,1:T(8,128)S(1)} fusion(f32[32,256,128]{2,0,1:T(8,128)S(1)} %copy-done, f32[16,4,256,128]{3,2,1,0:T(8,128)S(1)} %fusion.120, pred[]{:T(512)S(6)} %compare.15, s32[16,4]{0,1:T(4,128)S(1)} %dynamic-slice_bitcast_fusion.9), kind=kOutput, calls=%fused_computation.22.clone.1 | convolution fusion | flops 807405568 | bytes 16777472 | tf_op jit(solution)/shard_map/while/body/eval_jaxpr/bjp,bjkd->pkd/dot_general | solution.py:58
  304.6 3.0 fusion.121
  309.8 10.7 %bitcast_add_fusion.3 = f32[32,256,128]{2,0,1:T(8,128)S(1)} fusion(f32[32,256,128]{2,0,1:T(8,128)S(1)} %copy-done, f32[16,4,256,128]{3,2,1,0:T(8,128)S(1)} %fusion.120, pred[]{:T(512)S(6)} %compare.15, s32[16,4]{0,1:T(4,128)S(1)} %dynamic-slice_bitcast_fusion.9), kind=kOutput, calls=%fused_computation.22.clone.1 | convolution fusion | flops 807405568 | bytes 16777472 | tf_op jit(solution)/shard_map/while/body/eval_jaxpr/bjp,bjkd->pkd/dot_general | solution.py:58
  322.5 6.0 %copy.210 = bf16[32,256,128]{2,1,0:T(8,128)(2,1)} copy(f32[32,256,128]{2,0,1:T(8,128)} %get-tuple-element.82) | data formatting | bytes 6291456 | tf_op jit(solution)/shard_map/while | solution.py:186
  328.5 4.6 %all-to-all-start.4 = ((bf16[64,2,32,128]{3,2,1,0:T(8,128)(2,1)}), bf16[64,2,32,128]{3,2,1,0:T(8,128)(2,1)S(1)}, u32[]{:S(2)}, u32[]{:S(2)}) async-start(bf16[64,2,32,128]{3,2,1,0:T(8,128)(2,1)} %bitcast.24), calls=%async_computation.4 | async-start | bytes 2097152 | tf_op jit(solution)/shard_map/all_to_all | solution.py:191
  333.2 28.1 %all-to-all-done.4 = bf16[64,2,32,128]{3,2,1,0:T(8,128)(2,1)S(1)} async-done(((bf16[64,2,32,128]{3,2,1,0:T(8,128)(2,1)}), bf16[64,2,32,128]{3,2,1,0:T(8,128)(2,1)S(1)}, u32[]{:S(2)}, u32[]{:S(2)}) %all-to-all-start.4) | async-done | bytes 1048608 | tf_op jit(solution)/shard_map/all_to_all | solution.py:191
  362.8 5.0 %fusion.60 = f32[16,32,128]{2,0,1:T(8,128)S(1)} fusion(f32[16,32,128]{2,0,1:T(8,128)S(1)} %fusion.75, f32[16,32]{0,1:T(8,128)S(1)} %add_rsqrt_fusion.1, bf16[16,32,128]{2,1,0:T(8,128)(2,1)S(1)} %copy-done.3), kind=kOutput, calls=%fused_computation.65 | output fusion | flops 524927 | bytes 657408 | tf_op jit(solution)/shard_map/mul | solution.py:18
  368.6 6.5 %fusion.56 = f32[32,64,128]{2,1,0:T(8,128)} fusion(bf16[32,64,128]{2,1,0:T(8,128)(2,1)} %reduce-scatter.2.cloned.1.call-done, f32[32,256,128]{2,1,0:T(8,128)} %get-tuple-element.251, s32[]{:T(128)S(6)} %select_n.69, f32[32,64]{1,0:T(8,128)S(1)} %constant_dynamic-slice_fusion), kind=kOutput, calls=%fused_computation.60 | output fusion | flops 1575039 | bytes 4203520 | tf_op jit(solution)/shard_map/mul | solution.py:18
  (227 shorter events, 128.4 us)
Async XLA Ops:
  7.2 33.6 %copy-start.2 = (bf16[32,256,128]{2,1,0:T(8,128)(2,1)S(1)}, bf16[32,256,128]{2,1,0:T(8,128)(2,1)}, u32[]{:S(2)}) copy-start(bf16[32,256,128]{2,1,0:T(8,128)(2,1)} %param.10) | copy-start | bytes 6291460
  7.7 2.2 copy-start.8
  9.1 18.4 %copy-start.7 = (s32[1024]{0:T(1024)}, s32[1024]{0:T(1024)S(1)}, u32[]{:S(2)}) copy-start(s32[1024]{0:T(1024)S(1)} %pad_clamp_fusion.1) | copy-start | bytes 12292
  9.2 18.2 %copy-start.4 = (pred[64,2]{1,0:T(8,128)(4,1)}, pred[64,2]{1,0:T(8,128)(4,1)S(1)}, u32[]{:S(2)}) copy-start(pred[64,2]{1,0:T(8,128)(4,1)S(1)} %reduce_or.21) | copy-start | bytes 388
  13.1 23.1 %all-to-all-start = ((s32[64,2,8]{2,1,0:T(2,128)}), s32[64,2,8]{2,1,0:T(2,128)S(1)}, u32[]{:S(2)}, u32[]{:S(2)}) async-start(s32[64,2,8]{2,1,0:T(2,128)} %copy.145), calls=%async_computation | async-start | bytes 131072 | tf_op jit(solution)/shard_map/all_to_all | solution.py:110
  26.4 9.8 %copy-start.5 = (pred[128,16]{0,1:T(8,128)(4,1)}, pred[128,16]{0,1:T(8,128)(4,1)S(1)}, u32[]{:S(2)}) copy-start(pred[128,16]{0,1:T(8,128)(4,1)S(1)} %fusion.74) | copy-start | bytes 6148
  36.2 32.6 %all-to-all-start.1 = ((bf16[64,2,32,128]{3,2,1,0:T(8,128)(2,1)}), bf16[64,2,32,128]{3,2,1,0:T(8,128)(2,1)S(1)}, u32[]{:S(2)}, u32[]{:S(2)}) async-start(bf16[64,2,32,128]{3,2,1,0:T(8,128)(2,1)} %bitcast.50), calls=%async_computation.1 | async-start | bytes 2097152 | tf_op jit(solution)/shard_map/all_to_all | solution.py:103
  108.3 16.5 %all-to-all-start.2 = ((f32[64,2,4]{2,1,0:T(2,128)}), f32[64,2,4]{2,1,0:T(2,128)S(1)}, u32[]{:S(2)}, u32[]{:S(2)}) async-start(f32[64,2,4]{2,1,0:T(2,128)} %bitcast.17), calls=%async_computation.2 | async-start | bytes 131072 | tf_op jit(solution)/shard_map/all_to_all | solution.py:142
  130.2 14.6 %all-to-all-start.3 = ((f32[64,2,4]{2,1,0:T(2,128)}), f32[64,2,4]{2,1,0:T(2,128)S(1)}, u32[]{:S(2)}, u32[]{:S(2)}) async-start(f32[64,2,4]{2,1,0:T(2,128)} %broadcast_select_fusion), calls=%async_computation.3 | async-start | bytes 131072 | tf_op jit(solution)/shard_map/all_to_all | solution.py:153
  134.6 234.0 %reduce-scatter.2.cloned.1.call-start = ((), (), s32[]{:S(2)}) async-start(), calls=%async_computation.6 | async-start | bytes 2621440 | tf_op jit(solution)/shard_map/reduce_scatter | solution.py:187
  152.3 2.2 copy-start
  165.3 2.0 copy-start.1
  174.5 2.2 copy-start
  187.4 2.0 copy-start.1
  196.7 2.2 copy-start
  209.6 2.0 copy-start.1
  218.8 2.2 copy-start
  231.8 2.0 copy-start.1
  241.0 2.2 copy-start
  254.0 2.0 copy-start.1
  263.2 2.2 copy-start
  276.1 2.0 copy-start.1
  285.4 2.2 copy-start
  298.3 2.0 copy-start.1
  307.6 2.2 copy-start
  320.5 2.0 copy-start.1
  328.5 33.9 %copy-start.6 = (pred[128,16]{0,1:T(8,128)(4,1)S(1)}, pred[128,16]{0,1:T(8,128)(4,1)}, u32[]{:S(2)}) copy-start(pred[128,16]{0,1:T(8,128)(4,1)} %copy-done.5) | copy-start | bytes 6148
  328.5 34.3 %copy-start.3 = (bf16[16,32,128]{2,1,0:T(8,128)(2,1)S(1)}, bf16[16,32,128]{2,1,0:T(8,128)(2,1)}, u32[]{:S(2)}) copy-start(bf16[16,32,128]{2,1,0:T(8,128)(2,1)} %param.9) | copy-start | bytes 393220
  328.5 32.8 %all-to-all-start.4 = ((bf16[64,2,32,128]{3,2,1,0:T(8,128)(2,1)}), bf16[64,2,32,128]{3,2,1,0:T(8,128)(2,1)S(1)}, u32[]{:S(2)}, u32[]{:S(2)}) async-start(bf16[64,2,32,128]{3,2,1,0:T(8,128)(2,1)} %bitcast.24), calls=%async_computation.4 | async-start | bytes 2097152 | tf_op jit(solution)/shard_map/all_to_all | solution.py:191
Sparse Core Ops, SparseCore 0:
  328.6 26.7 reduce-scatter.1
where the time goes:
time: 383 us; the launch traced here: 382 us
  matrix products  182 us (48%)
  waiting for transfers between devices  75.4 us (20%)
  local copies, waits for them, and re-layouts  53 us (14%)
  starting transfers between devices  33 us (9%)
  other arithmetic  23.6 us (6%)
  between operations  14.3 us (4%)
    dot_general x8, matrix products, add_rows(): jnp.einsum('bjp,bjkd->pkd', selector, passage_grad, precision=lax.Precisi...  85.8 us
    all_to_all x1, waiting for transfers between devices, per_device(): lax.all_to_all(query_slots.reshape(pool_size, capacity, query_len, featur...  28.1 us
    dot_general x8, matrix products, both_block(): jnp.einsum('bjik,bjkd->bid', dsoft, candidates, preferred_element_type=jn...  23.6 us
    while x40, local copies, waits for them, and re-layouts  22.9 us
    all_to_all x1, waiting for transfers between devices, per_device(): lax.all_to_all(q_slots.reshape(pool_size, capacity, query_len, feature_di...  21.7 us
    dot_general x8, matrix products, forward_block(): jnp.einsum('bid,bjkd->bjik', queries, candidates, preferred_element_type=...  20.9 us
    dot_general x16, matrix products, pick_rows(): jnp.einsum('bjp,pkd->bjkd', selector, table, preferred_element_type=jnp.f...  20.6 us
    dot_general x8, matrix products, both_block(): jnp.einsum('bid,bjkd->bjik', queries, candidates, preferred_element_type=...  18.1 us
  transfers between devices with their start and end apart: 6, of which 5 were waited for; matrix products, arithmetic and copies ran while one was open for 5% of the time, Pallas kernels for 0%

commit v1 on v0

v1 whole, which is shorter than its diff:
```python
import math

import jax
import jax.numpy as jnp
from jax import lax
from jax.experimental import pallas as pl
from jax.experimental.pallas import tpu as pltpu
from jax.sharding import PartitionSpec as P

MESH = pl.DeviceIdType.MESH
f32, bf16, i32 = jnp.float32, jnp.bfloat16, jnp.int32

TEMPER = 0.05
LOSS_SCALE = 16.0
EPSILON = 1e-06

NP = 64
NR = 4
CAP = 2
NQ = 16
QT = 32
DIM = 128
PT = 256
NPASS = 32
GROUPS = 4
WIDTH = 4
SLOTS = NP * CAP
TILE = 8
NTILES = (SLOTS * WIDTH + NPASS * (TILE - 1)) // TILE
SHARE = PT // NR
RS_CHUNK = 8
HIGH = lax.Precision.HIGHEST


def iota(shape, dim):
    return lax.broadcasted_iota(i32, shape, dim)


def hot(cond, dtype=f32):
    return jnp.where(cond, 1.0, 0.0).astype(dtype)


def index(x, bound):
    return jnp.clip(x.astype(i32), 0, bound - 1)


def dot(a, b):
    return jnp.dot(a.astype(bf16), b.astype(bf16), preferred_element_type=f32)


def dot_nt(a, b):
    return lax.dot_general(
        a.astype(bf16), b.astype(bf16), (((1,), (1,)), ((), ())), preferred_element_type=f32
    )


def hdot(a, b):
    return jnp.dot(a, b, preferred_element_type=f32, precision=HIGH)


def hdot_nt(a, b):
    return lax.dot_general(
        a, b, (((1,), (1,)), ((), ())), preferred_element_type=f32, precision=HIGH
    )


def kernel(
    q_ref, p_any, meta_ref,
    loss_ref, gq_ref, gp_ref,
    p_raw, p_low, q_low, q_send, q_recv, meta_send, meta_recv, sc_send, sc_recv, w_send, w_recv,
    rows_ref, rhs_ref, soft_ref, a_ref, qn_ref, ret_send, ret_recv, rs_send, rs_recv,
    tbla_v, tblb_v, wt_v, tbla, tblb, wt,
    sem_p, sem_tbl, q_ss, q_rs, m_ss, m_rs, s_ss, s_rs, w_ss, w_rs, r_ss, r_rs, x_ss, x_rs,
):
    me = lax.axis_index("pool")
    rep = lax.axis_index("rep")

    def wait_bytes(ref, sem):
        pltpu.make_async_copy(ref, ref, sem).wait()

    def to_pool(src, dst, ss, rs, peer):
        return pltpu.make_async_remote_copy(
            src_ref=src, dst_ref=dst, send_sem=ss, recv_sem=rs, device_id=(peer, rep), device_id_type=MESH
        )

    p_copy = pltpu.make_async_copy(p_any, p_raw, sem_p)
    p_copy.start()

    barrier = pltpu.get_barrier_semaphore()

    def greet(d, _):
        pl.semaphore_signal(
            barrier, inc=1, device_id=(lax.rem(me + d, NP), rep), device_id_type=MESH
        )
        return 0

    lax.fori_loop(1, NP, greet, 0)
    for d in range(1, NR):
        pl.semaphore_signal(
            barrier, inc=1, device_id=(me, lax.rem(rep + d, NR)), device_id_type=MESH
        )

    for a in range(NQ):
        x = q_ref[a].astype(f32)
        inv = lax.rsqrt(jnp.sum(x * x, axis=-1, keepdims=True) + EPSILON)
        q_low[a] = (x * inv).astype(bf16)

    npair = GROUPS * NQ
    mf = meta_ref[...].astype(f32)
    cols = mf.shape[1]
    lane_m = iota((NQ, cols), 1)
    own_col = jnp.concatenate(
        [
            jnp.sum(jnp.where(lane_m == g, mf, 0.0), axis=1, keepdims=True)
            for g in range(GROUPS)
        ],
        axis=0,
    )
    src_r, dst_c = iota((cols, 128), 0), iota((cols, 128), 1)
    loc_w = jnp.concatenate(
        [
            dot(mf, hot((src_r == GROUPS + WIDTH * g + dst_c) & (dst_c < WIDTH)))
            for g in range(GROUPS)
        ],
        axis=0,
    )
    mask_w = [
        dot(mf, hot((src_r == GROUPS + GROUPS * WIDTH + WIDTH * g + dst_c) & (dst_c < WIDTH)))
        for g in range(GROUPS)
    ]
    ra, ca = iota((npair, npair), 0), iota((npair, npair), 1)
    own_row = jnp.sum(jnp.where(ra == ca, own_col, 0.0), axis=0, keepdims=True)
    same = own_col == own_row
    rank_col = jnp.sum(hot(same & (ca % NQ < ra % NQ)), axis=1, keepdims=True)
    rank_row = jnp.sum(hot(same & (ra % NQ < ca % NQ)), axis=0, keepdims=True)
    slot_col = CAP * own_col + rank_col
    slot_row = CAP * own_row + rank_row
    st = hot(slot_col == iota((npair, SLOTS), 1).astype(f32))
    s_hot = hot(slot_row == iota((SLOTS, npair), 0).astype(f32))
    qidx_row = jnp.sum(
        st * (iota((npair, SLOTS), 0) % NQ).astype(f32), axis=0, keepdims=True
    )
    slot_wide = jnp.sum(
        jnp.where(iota((npair, 128), 0) == iota((npair, 128), 1), slot_col, 0.0),
        axis=0, keepdims=True,
    )
    tbla_v[0:8, :] = index(jnp.broadcast_to(qidx_row, (8, 128)), NQ)
    tbla_v[8:16, :] = index(jnp.broadcast_to(slot_wide, (8, 128)), SLOTS)
    tbla_copy = pltpu.make_async_copy(tbla_v, tbla, sem_tbl)
    tbla_copy.start()
    loc_slots = dot(s_hot, loc_w)
    for peer in range(NP):
        meta_send[peer] = loc_slots[CAP * peer : CAP * (peer + 1), :]
    tbla_copy.wait()
    pl.semaphore_wait(barrier, NP - 1 + NR - 1)

    def send_meta(d, _):
        peer = lax.rem(me + d, NP)
        to_pool(meta_send.at[peer], meta_recv.at[me], m_ss, m_rs, peer).start()
        return 0

    lax.fori_loop(1, NP, send_meta, 0)
    meta_recv[me] = meta_send[me]

    def send_q(d, _):
        peer = lax.rem(me + d, NP)
        for k in range(CAP):
            q_send[CAP * peer + k] = q_low[tbla[0, CAP * peer + k]]
        to_pool(
            q_send.at[pl.ds(CAP * peer, CAP)], q_recv.at[pl.ds(CAP * me, CAP)], q_ss, q_rs, peer
        ).start()
        return 0

    lax.fori_loop(1, NP, send_q, 0)
    for k in range(CAP):
        q_recv[CAP * me + k] = q_low[tbla[0, CAP * me + k]]

    p_copy.wait()

    def norm_passage(p, _):
        x = p_raw[p].astype(f32)
        inv = lax.rsqrt(jnp.sum(x * x, axis=-1, keepdims=True) + EPSILON)
        p_low[p] = (x * inv).astype(bf16)
        return 0

    lax.fori_loop(0, NPASS, norm_passage, 0)

    wait_bytes(meta_recv.at[pl.ds(0, NP - 1)], m_rs)
    for peer in range(NP):
        rows_ref[CAP * peer : CAP * (peer + 1), :] = meta_recv[peer]
    loc_r = rows_ref[...]
    r_i, c_i = iota((128, 128), 0), iota((128, 128), 1)
    pc, jc, pr, jr = c_i % NPASS, c_i // NPASS, r_i % NPASS, r_i // NPASS
    one_hot = hot(dot(loc_r, hot((r_i == jc) & (r_i < WIDTH))) == pc.astype(f32))
    before = dot(hot(c_i < r_i), one_hot)
    total = jnp.broadcast_to(jnp.sum(one_hot, axis=0, keepdims=True), (8, 128))
    base = dot(total, hot((pr == pc) & (jr < jc)))[0:1, :]
    tiles = jnp.floor((dot(total, hot(pr == pc)) + (TILE - 1)) * (1.0 / TILE))
    offset = dot(tiles, hot((jr == 0) & (pr < pc)))
    rank = base + before
    rank_tile = jnp.floor(rank * (1.0 / TILE))
    x_tile = one_hot * (offset[0:1, :] + rank_tile)
    x_rest = one_hot * (rank - TILE * rank_tile)
    fold = hot((c_i == jr) & (c_i < WIDTH))
    tile_c = dot(x_tile, fold)
    rest_c = dot(x_rest, fold)
    fold_row = hot(iota((8, 128), 0) == iota((8, 128), 1) // NPASS)
    tile_r = dot_nt(fold_row, x_tile)
    rest_r = dot_nt(fold_row, x_rest)
    loc_rows = dot_nt(hot(iota((8, 128), 0) == iota((8, 128), 1)), loc_r)
    sub8 = iota((8, 128), 0).astype(f32)
    slot_ids = iota((8, 128), 1).astype(f32)
    table = jnp.zeros((16, 128), f32)
    for j in range(WIDTH):
        rest_j = rest_r[j : j + 1, :]
        lhs = jnp.concatenate(
            [
                jnp.where(rest_j == sub8, slot_ids, 0.0),
                jnp.where(rest_j == 0.0, loc_rows[j : j + 1, :], jnp.zeros((8, 128), f32)),
            ],
            axis=0,
        )
        rhs = hot(tile_c[:, j : j + 1] == c_i.astype(f32))
        rhs_ref[j] = rhs
        table = table + dot(lhs, rhs)
    tblb_v[0:8, :] = index(table[0:8], SLOTS)
    tblb_v[8:16, :] = index(table[8:16], NPASS)
    tblb_v[16:24, :] = index(TILE * tile_r + rest_r, NTILES * TILE)
    tblb_v[24:32, :] = index(offset + tiles - 1.0, NTILES)
    tblb_v[32:40, :] = index(tiles, 2)
    tblb_copy = pltpu.make_async_copy(tblb_v, tblb, sem_tbl)
    tblb_copy.start()
    tblb_copy.wait()

    wait_bytes(q_recv.at[pl.ds(0, CAP * (NP - 1))], q_rs)
    ones = jnp.ones((PT, DIM), bf16)
    lane8 = iota((8, 128), 1)

    def forward_tile(t, scores):
        p_tile = p_low[tblb[8, t]]
        q_tile = jnp.concatenate([q_recv[tblb[r, t]] for r in range(TILE)], axis=0)
        sims = lax.dot_general(
            q_tile, p_tile, (((1,), (1,)), ((), ())), preferred_element_type=f32
        )
        soft = jnp.exp2(sims * (math.log2(math.e) / TEMPER)).astype(bf16)
        soft_ref[t] = soft
        both = jnp.dot(
            soft, jnp.concatenate([p_tile, ones], axis=1), preferred_element_type=f32
        )
        sums = both[:, DIM:]
        inv = 1.0 / sums
        a_ref[pl.ds(TILE * t, TILE)] = (both[:, :DIM] * inv).reshape(TILE, QT, DIM)
        qn_ref[t] = q_tile.astype(f32) * inv
        means = (sums * (1.0 / PT)).reshape(TILE, QT // 8, 8, DIM)
        product = means[:, 0]
        for i in range(1, QT // 8):
            product = product * means[:, i]
        logs = jnp.sum(jnp.log(product), axis=1)
        score = TEMPER * (logs + QT * math.log(PT))
        return jnp.where(lane8 == t, score, scores)

    scores = lax.fori_loop(0, NTILES, forward_tile, jnp.zeros((8, 128), f32))

    sc = jnp.zeros((SLOTS, 128), f32)
    lane_s = iota((SLOTS, 128), 1)
    lane_r = iota((SLOTS, 8), 1).astype(f32)
    for j in range(WIDTH):
        picked = hdot_nt(rhs_ref[j], scores)
        col = jnp.sum(
            jnp.where(rest_c[:, j : j + 1] == lane_r, picked, 0.0), axis=1, keepdims=True
        )
        sc = jnp.where(lane_s == j, col, sc)
    for peer in range(NP):
        sc_send[peer] = sc[CAP * peer : CAP * (peer + 1), :]

    def send_sc(d, _):
        peer = lax.rem(me + d, NP)
        to_pool(sc_send.at[peer], sc_recv.at[me], s_ss, s_rs, peer).start()
        return 0

    lax.fori_loop(1, NP, send_sc, 0)
    sc_recv[me] = sc_send[me]
    wait_bytes(sc_recv.at[pl.ds(0, NP - 1)], s_rs)
    for peer in range(NP):
        rows_ref[CAP * peer : CAP * (peer + 1), :] = sc_recv[peer]

    own_scores = hdot(st, rows_ref[...])
    lane_q = iota((NQ, 128), 1)
    denom = jnp.zeros((NQ, 1), f32)
    exps = []
    for g in range(GROUPS):
        valid = mask_w[g]
        if g == 0:
            valid = jnp.where(lane_q == 0, 1.0, valid)
        e = jnp.exp(own_scores[NQ * g : NQ * (g + 1), :]) * valid
        exps.append(e)
        denom = denom + jnp.sum(e, axis=1, keepdims=True)
    losses = jnp.log(denom) - own_scores[0:NQ, 0:1]
    loss_ref[...] = jnp.sum(
        jnp.where(iota((NQ, NQ), 0) == iota((NQ, NQ), 1), losses, 0.0), axis=0, keepdims=True
    )
    dscore = [LOSS_SCALE * (e / denom) for e in exps]
    dscore[0] = dscore[0] - jnp.where(lane_q == 0, LOSS_SCALE, 0.0)
    w_slots = hdot(s_hot, jnp.concatenate(dscore, axis=0))
    for peer in range(NP):
        w_send[peer] = w_slots[CAP * peer : CAP * (peer + 1), :]

    def send_w(d, _):
        peer = lax.rem(me + d, NP)
        to_pool(w_send.at[peer], w_recv.at[me], w_ss, w_rs, peer).start()
        return 0

    lax.fori_loop(1, NP, send_w, 0)
    w_recv[me] = w_send[me]
    wait_bytes(w_recv.at[pl.ds(0, NP - 1)], w_rs)
    for peer in range(NP):
        rows_ref[CAP * peer : CAP * (peer + 1), :] = w_recv[peer]

    w_rows = hdot_nt(hot(iota((8, 128), 0) == iota((8, 128), 1)), rows_ref[...])
    w_tile = jnp.zeros((8, 128), f32)
    for j in range(WIDTH):
        lhs = jnp.where(rest_r[j : j + 1, :] == sub8, w_rows[j : j + 1, :], 0.0)
        w_tile = w_tile + hdot(lhs, rhs_ref[j])
    wt_v[...] = w_tile
    wt_copy = pltpu.make_async_copy(wt_v, wt, sem_tbl)
    wt_copy.start()
    wt_copy.wait()

    def group_grad(s):
        acc = jnp.zeros((QT, DIM), f32)
        for j in range(WIDTH):
            pos = tblb[16 + j, s]
            acc = acc + wt[pos & (TILE - 1), pos >> 3] * a_ref[pos]
        return acc.astype(bf16)

    def send_ret(d, _):
        peer = lax.rem(me + d, NP)
        for k in range(CAP):
            ret_send[CAP * peer + k] = group_grad(CAP * peer + k)
        to_pool(
            ret_send.at[pl.ds(CAP * peer, CAP)], ret_recv.at[pl.ds(CAP * me, CAP)], r_ss, r_rs, peer
        ).start()
        return 0

    lax.fori_loop(1, NP, send_ret, 0)
    for k in range(CAP):
        ret_recv[CAP * me + k] = group_grad(CAP * me + k)

    def passage_tile(t, _):
        qs = jnp.concatenate(
            [
                (qn_ref[t, QT * r : QT * (r + 1), :] * wt[r, t]).astype(bf16)
                for r in range(TILE)
            ],
            axis=0,
        )
        grad = lax.dot_general(
            qs, soft_ref[t], (((0,), (0,)), ((), ())), preferred_element_type=f32
        )
        halves = jnp.concatenate([grad[:, :128], grad[:, 128:]], axis=0).reshape(TILE, QT, DIM)
        prev = jnp.maximum(t - 1, 0)
        again = (t > 0) & (tblb[8, t] == tblb[8, prev])
        keep = jnp.where(again, 1.0, 0.0).astype(f32)
        a_ref[pl.ds(TILE * t, TILE)] = halves + keep * a_ref[pl.ds(TILE * prev, TILE)]
        return 0

    lax.fori_loop(0, NTILES, passage_tile, 0)

    for chunk in range(NPASS // RS_CHUNK):

        def cut_passage(i, _):
            p = chunk * RS_CHUNK + i
            last = TILE * tblb[24, p]
            used = tblb[32, p].astype(f32)
            for half in range(2):
                x = jnp.concatenate(
                    [a_ref[last + 4 * half + m] for m in range(4)], axis=0
                )
                y = (x * used).T.astype(bf16)
                for part in range(2):
                    rs_send[2 * half + part, p] = y[SHARE * part : SHARE * (part + 1), :]
            return 0

        lax.fori_loop(0, RS_CHUNK, cut_passage, 0)
        rows = pl.ds(chunk * RS_CHUNK, RS_CHUNK)
        for d in range(1, NR):
            target = lax.rem(rep + d, NR)
            pltpu.make_async_remote_copy(
                src_ref=rs_send.at[target, rows],
                dst_ref=rs_recv.at[d - 1, rows],
                send_sem=x_ss,
                recv_sem=x_rs,
                device_id=(me, target),
                device_id_type=MESH,
            ).start()

    wait_bytes(ret_recv.at[pl.ds(0, CAP * (NP - 1))], r_rs)

    def finish_query(a, _):
        x = q_ref[a].astype(f32)
        inv = lax.rsqrt(jnp.sum(x * x, axis=-1, keepdims=True) + EPSILON)
        unit = x * inv
        up = jnp.zeros((QT, DIM), f32)
        for g in range(GROUPS):
            up = up + ret_recv[tbla[8, NQ * g + a]].astype(f32)
        gq_ref[a] = inv * (up - unit * jnp.sum(unit * up, axis=-1, keepdims=True))
        return 0

    lax.fori_loop(0, NQ, finish_query, 0)

    wait_bytes(rs_recv, x_rs)
    start = pl.multiple_of(rep * SHARE, SHARE)

    def finish_passage(p, _):
        x = p_raw[p, pl.ds(start, SHARE), :].astype(f32)
        inv = lax.rsqrt(jnp.sum(x * x, axis=-1, keepdims=True) + EPSILON)
        unit = x * inv
        up = rs_send[rep, p].astype(f32)
        for d in range(NR - 1):
            up = up + rs_recv[d, p].astype(f32)
        gp_ref[p] = inv * (up - unit * jnp.sum(unit * up, axis=-1, keepdims=True))
        return 0

    lax.fori_loop(0, NPASS, finish_passage, 0)

    wait_bytes(meta_send.at[pl.ds(0, NP - 1)], m_ss)
    wait_bytes(q_send.at[pl.ds(0, CAP * (NP - 1))], q_ss)
    wait_bytes(sc_send.at[pl.ds(0, NP - 1)], s_ss)
    wait_bytes(w_send.at[pl.ds(0, NP - 1)], w_ss)
    wait_bytes(ret_send.at[pl.ds(0, CAP * (NP - 1))], r_ss)
    wait_bytes(rs_recv, x_ss)


def per_device(query_vecs, passage_vecs, owner_ids, local_ids, cand_mask):
    meta = jnp.concatenate(
        [owner_ids, local_ids.reshape(NQ, GROUPS * WIDTH), cand_mask], axis=1
    )
    vmem = pl.BlockSpec(memory_space=pltpu.VMEM)
    rows = pltpu.VMEM((NP, CAP, 128), f32)
    dma = pltpu.SemaphoreType.DMA
    loss, grad_query, grad_passage = pl.pallas_call(
        kernel,
        out_shape=(
            jax.ShapeDtypeStruct((1, NQ), f32),
            jax.ShapeDtypeStruct((NQ, QT, DIM), f32),
            jax.ShapeDtypeStruct((NPASS, SHARE, DIM), f32),
        ),
        in_specs=[vmem, pl.BlockSpec(memory_space=pl.ANY), vmem],
        out_specs=[vmem, vmem, vmem],
        scratch_shapes=[
            pltpu.VMEM((NPASS, PT, DIM), bf16),
            pltpu.VMEM((NPASS, PT, DIM), bf16),
            pltpu.VMEM((NQ, QT, DIM), bf16),
            pltpu.VMEM((SLOTS, QT, DIM), bf16),
            pltpu.VMEM((SLOTS, QT, DIM), bf16),
            rows, rows, rows, rows, rows, rows,
            pltpu.VMEM((SLOTS, 128), f32),
            pltpu.VMEM((WIDTH, 128, 128), f32),
            pltpu.VMEM((NTILES, TILE * QT, PT), bf16),
            pltpu.VMEM((NTILES * TILE, QT, DIM), f32),
            pltpu.VMEM((NTILES, TILE * QT, DIM), f32),
            pltpu.VMEM((SLOTS, QT, DIM), bf16),
            pltpu.VMEM((SLOTS, QT, DIM), bf16),
            pltpu.VMEM((NR, NPASS, SHARE, DIM), bf16),
            pltpu.VMEM((NR - 1, NPASS, SHARE, DIM), bf16),
            pltpu.VMEM((16, 128), i32),
            pltpu.VMEM((40, 128), i32),
            pltpu.VMEM((8, 128), f32),
            pltpu.SMEM((16, 128), i32),
            pltpu.SMEM((40, 128), i32),
            pltpu.SMEM((8, 128), f32),
        ]
        + [dma(())] * 14,
        compiler_params=pltpu.CompilerParams(
            collective_id=0, has_side_effects=True, vmem_limit_bytes=62 * 1024 * 1024
        ),
    )(query_vecs, passage_vecs, meta)
    return (loss.reshape(NQ), grad_query, grad_passage)


def solution(mesh):
    return jax.shard_map(
        per_device,
        mesh=mesh,
        in_specs=(
            P(("pool", "rep"), None, None),
            P("pool", None, None),
            P(("pool", "rep"), None),
            P(("pool", "rep"), None, None),
            P(("pool", "rep"), None),
        ),
        out_specs=(P(("pool", "rep")), P(("pool", "rep"), None, None), P("pool", "rep", None)),
        check_vma=False,
    )
```

time: 383 us -> 152 us (0.40)
  matrix products: 182 us -> 0 us
  Pallas kernels: 0 us -> 143 us
  waiting for transfers between devices: 75.4 us -> 0 us
  local copies, waits for them, and re-layouts: 53 us -> 6.62 us
  starting transfers between devices: 33 us -> 0 us
  other arithmetic: 23.6 us -> 1.37 us
  between operations: 14.3 us -> 0.64 us
    dot_general x58 -> x0, matrix products: 182 us -> none  [the longest x8 85.8 us: add_rows(): jnp.einsum('bjp,bjkd->pkd', selector, passage_grad, precision=lax.Precisi...]
    pallas_call x0 -> x1, Pallas kernels: none -> 143 us  [per_device(): pl.pallas_call(kernel, out_shape=(jax.ShapeDtypeStruct((1, NQ), f32), jax...]
    all_to_all x5 -> x0, waiting for transfers between devices: 75.4 us -> none  [the longest x1 28.1 us: per_device(): lax.all_to_all(query_slots.reshape(pool_size, capacity, query_len, featur...]
    all_to_all x5 -> x0, starting transfers between devices: 33 us -> none  [the longest x1 13 us: per_device(): lax.all_to_all(meta.reshape(pool_size, capacity, meta.shape[1]), 'pool',...]
    while x44 -> x0, local copies, waits for them, and re-layouts: 31.7 us -> none
    mul x14 -> x0, other arithmetic: 15.4 us -> none  [the longest x2 11.5 us: unit_backward(): unit_vecs * jnp.sum(unit_vecs * upstream, axis=-1, keepdims=True)]
    eq x17 -> x0, local copies, waits for them, and re-layouts: 10.9 us -> none  [the longest x16 10.8 us: one_hot_rows(): return (cand_rows[..., None] == table_ids).astype(dtype)]
    reduce_sum x13 -> x0, other arithmetic: 4.16 us -> none  [the longest x2 2.2 us: normalize(): jnp.sum(widened * widened, axis=-1, keepdims=True) + epsilon]
  transfers between devices with their start and end apart: 6 -> 0, of which waited for: 5 -> 0; matrix products, arithmetic and copies ran while one was open for 5% -> 0% of each run, Pallas kernels for 0% -> 0%
where the time goes in v1:
time: 152 us; the launch traced here: 151 us
  Pallas kernels  143 us (94%)
  local copies, waits for them, and re-layouts  6.62 us (4%)
    pallas_call x1, Pallas kernels, per_device(): pl.pallas_call(kernel, out_shape=(jax.ShapeDtypeStruct((1, NQ), f32), jax...  143 us
    unnamed x4, local copies, waits for them, and re-layouts  5.86 us

profile of v1, /device:TPU:1, one launch (start us, length us, event | category | flops | bytes accessed | tf_op | source)
XLA Modules:
  0.0 151.5 jit_solution(12336076094642120655)
XLA Ops:
  0.6 0.8 copy.10
  1.4 0.8 copy.11
  2.2 1.4 pad_add_fusion.meta_ref
  3.5 142.8 %shard_map.76 = (f32[1,16]{1,0:T(1,128)}, f32[16,32,128]{2,1,0:T(8,128)}, f32[32,64,128]{2,1,0:T(8,128)}) custom-call(bf16[16,32,128]{2,1,0:T(8,128)(2,1)} %q_ref.1, bf16[32,256,128]{2,1,0:T(8,128)(2,1)} %p_any.1, s32[16,36]{1,0:T(8,128)} %pad_add_fusion.meta_ref), custom_call_target="tpu_custom_call" | custom-call | tf_op jit(solution)/shard_map/pallas_call | solution.py:441
  146.4 1.1 copy.15
  147.5 1.7 %copy.16 = f32[16,32,128]{2,1,0:T(8,128)} copy(f32[16,32,128]{2,1,0:T(8,128)} %get-tuple-element.13) | data formatting | bytes 524288
  149.2 2.3 %copy.17 = f32[32,64,128]{2,1,0:T(8,128)} copy(f32[32,64,128]{2,1,0:T(8,128)} %get-tuple-element.14) | data formatting | bytes 2097152

commit v2 on v1

--- a/solution.py
+++ b/solution.py
@@ -29,6 +29,7 @@
 NTILES = (SLOTS * WIDTH + NPASS * (TILE - 1)) // TILE
 SHARE = PT // NR
 RS_CHUNK = 8
+UNROLL = 23
 HIGH = lax.Precision.HIGHEST
 
 
@@ -183,7 +184,7 @@
         p_low[p] = (x * inv).astype(bf16)
         return 0
 
-    lax.fori_loop(0, NPASS, norm_passage, 0)
+    lax.fori_loop(0, NPASS, norm_passage, 0, unroll=2)
 
     wait_bytes(meta_recv.at[pl.ds(0, NP - 1)], m_rs)
     for peer in range(NP):
@@ -259,7 +260,7 @@
         score = TEMPER * (logs + QT * math.log(PT))
         return jnp.where(lane8 == t, score, scores)
 
-    scores = lax.fori_loop(0, NTILES, forward_tile, jnp.zeros((8, 128), f32))
+    scores = lax.fori_loop(0, NTILES, forward_tile, jnp.zeros((8, 128), f32), unroll=UNROLL)
 
     sc = jnp.zeros((SLOTS, 128), f32)
     lane_s = iota((SLOTS, 128), 1)
@@ -346,7 +347,7 @@
     for k in range(CAP):
         ret_recv[CAP * me + k] = group_grad(CAP * me + k)
 
-    def passage_tile(t, _):
+    def passage_tile(t, acc):
         qs = jnp.concatenate(
             [
                 (qn_ref[t, QT * r : QT * (r + 1), :] * wt[r, t]).astype(bf16)
@@ -357,14 +358,15 @@
         grad = lax.dot_general(
             qs, soft_ref[t], (((0,), (0,)), ((), ())), preferred_element_type=f32
         )
-        halves = jnp.concatenate([grad[:, :128], grad[:, 128:]], axis=0).reshape(TILE, QT, DIM)
+        halves = jnp.concatenate([grad[:, :128], grad[:, 128:]], axis=0)
         prev = jnp.maximum(t - 1, 0)
         again = (t > 0) & (tblb[8, t] == tblb[8, prev])
         keep = jnp.where(again, 1.0, 0.0).astype(f32)
-        a_ref[pl.ds(TILE * t, TILE)] = halves + keep * a_ref[pl.ds(TILE * prev, TILE)]
-        return 0
-
-    lax.fori_loop(0, NTILES, passage_tile, 0)
+        acc = halves + keep * acc
+        a_ref[pl.ds(TILE * t, TILE)] = acc.reshape(TILE, QT, DIM)
+        return acc
+
+    lax.fori_loop(0, NTILES, passage_tile, jnp.zeros((PT, DIM), f32), unroll=UNROLL)
 
     for chunk in range(NPASS // RS_CHUNK):
 
@@ -381,7 +383,7 @@
                     rs_send[2 * half + part, p] = y[SHARE * part : SHARE * (part + 1), :]
             return 0
 
-        lax.fori_loop(0, RS_CHUNK, cut_passage, 0)
+        lax.fori_loop(0, RS_CHUNK, cut_passage, 0, unroll=RS_CHUNK)
         rows = pl.ds(chunk * RS_CHUNK, RS_CHUNK)
         for d in range(1, NR):
             target = lax.rem(rep + d, NR)
@@ -406,7 +408,7 @@
         gq_ref[a] = inv * (up - unit * jnp.sum(unit * up, axis=-1, keepdims=True))
         return 0
 
-    lax.fori_loop(0, NQ, finish_query, 0)
+    lax.fori_loop(0, NQ, finish_query, 0, unroll=4)
 
     wait_bytes(rs_recv, x_rs)
     start = pl.multiple_of(rep * SHARE, SHARE)
@@ -421,7 +423,7 @@
         gp_ref[p] = inv * (up - unit * jnp.sum(unit * up, axis=-1, keepdims=True))
         return 0
 
-    lax.fori_loop(0, NPASS, finish_passage, 0)
+    lax.fori_loop(0, NPASS, finish_passage, 0, unroll=4)
 
     wait_bytes(meta_send.at[pl.ds(0, NP - 1)], m_ss)
     wait_bytes(q_send.at[pl.ds(0, CAP * (NP - 1))], q_ss)

time: 152 us -> 106 us (0.70)
  Pallas kernels: 143 us -> 96.9 us
    pallas_call x1, Pallas kernels: 143 us -> 96.9 us  [per_device(): pl.pallas_call(kernel, out_shape=(jax.ShapeDtypeStruct((1, NQ), f32), jax...]
where the time goes in v2:
time: 106 us; the launch traced here: 105 us
  Pallas kernels  96.9 us (91%)
  local copies, waits for them, and re-layouts  6.62 us (6%)
  other arithmetic  1.37 us (1%)
    pallas_call x1, Pallas kernels, per_device(): pl.pallas_call(kernel, out_shape=(jax.ShapeDtypeStruct((1, NQ), f32), jax...  96.9 us
    unnamed x4, local copies, waits for them, and re-layouts  5.86 us

profile of v2, /device:TPU:1, one launch (start us, length us, event | category | flops | bytes accessed | tf_op | source)
XLA Modules:
  0.0 105.5 jit_solution(10620529272862598393)
XLA Ops:
  0.6 0.8 copy.10
  1.4 0.8 copy.11
  2.2 1.4 %pad_add_fusion.meta_ref = s32[16,36]{1,0:T(8,128)} fusion(s32[16,16]{1,0:T(8,128)} %param.9, s32[16,16]{1,0:T(8,128)S(1)} %copy.11, s32[16,4]{1,0:T(8,128)S(1)} %copy.10), kind=kLoop, calls=%fused_computation | loop fusion | flops 1152 | bytes 4608 | tf_op jit(solution)/shard_map/concatenate | solution.py:437
  3.5 96.9 %shard_map.76 = (f32[1,16]{1,0:T(1,128)}, f32[16,32,128]{2,1,0:T(8,128)}, f32[32,64,128]{2,1,0:T(8,128)}) custom-call(bf16[16,32,128]{2,1,0:T(8,128)(2,1)} %q_ref.1, bf16[32,256,128]{2,1,0:T(8,128)(2,1)} %p_any.1, s32[16,36]{1,0:T(8,128)} %pad_add_fusion.meta_ref), custom_call_target="tpu_custom_call" | custom-call | tf_op jit(solution)/shard_map/pallas_call | solution.py:443
  100.4 1.1 %copy.15 = f32[16]{0:T(128)} copy(f32[16]{0:T(128)} %bitcast.3) | data formatting | bytes 128
  101.5 1.7 %copy.16 = f32[16,32,128]{2,1,0:T(8,128)} copy(f32[16,32,128]{2,1,0:T(8,128)} %get-tuple-element.13) | data formatting | bytes 524288
  103.2 2.3 %copy.17 = f32[32,64,128]{2,1,0:T(8,128)} copy(f32[32,64,128]{2,1,0:T(8,128)} %get-tuple-element.14) | data formatting | bytes 2097152

commit v3 on v2

--- a/solution.py
+++ b/solution.py
@@ -16,6 +16,8 @@
 
 NP = 64
 NR = 4
+NZ = 8
+NC = NP // NZ
 CAP = 2
 NQ = 16
 QT = 32
@@ -66,15 +68,18 @@
 
 
 def kernel(
-    q_ref, p_any, meta_ref,
+    q_ref, p_any, own_ref, loc_ref, mask_ref,
     loss_ref, gq_ref, gp_ref,
-    p_raw, p_low, q_low, q_send, q_recv, meta_send, meta_recv, sc_send, sc_recv, w_send, w_recv,
+    p_raw, p_low, q_low, plus1, plus2, plus3, minus1, minus2, minus3, far, q_send, q_recv,
+    m_a, m_b, m_c, s_a, s_b, s_c, w_a, w_b, w_c,
     rows_ref, rhs_ref, soft_ref, a_ref, qn_ref, ret_send, ret_recv, rs_send, rs_recv,
-    tbla_v, tblb_v, wt_v, tbla, tblb, wt,
-    sem_p, sem_tbl, q_ss, q_rs, m_ss, m_rs, s_ss, s_rs, w_ss, w_rs, r_ss, r_rs, x_ss, x_rs,
+    tbla_v, tblm_v, tblb_v, wt_v, tbla, tblm, tblb, wt,
+    sem_p, sem_tbl, hop_s, plus_r, minus_r, q_ss, q_rs, m_sem, s_sem, w_sem, r_ss, r_rs, x_ss, x_rs,
 ):
     me = lax.axis_index("pool")
     rep = lax.axis_index("rep")
+    z = lax.div(me, NC)
+    c = lax.rem(me, NC)
 
     def wait_bytes(ref, sem):
         pltpu.make_async_copy(ref, ref, sem).wait()
@@ -84,18 +89,45 @@
             src_ref=src, dst_ref=dst, send_sem=ss, recv_sem=rs, device_id=(peer, rep), device_id_type=MESH
         )
 
+    def along_z(e):
+        return NC * lax.rem(z + NZ + e, NZ) + c
+
+    def in_plane(e):
+        return NC * z + lax.rem(c + e, NC)
+
+    def first_hop(send, mid, sems):
+        for e in range(1, NZ):
+            target = lax.rem(z + e, NZ)
+            to_pool(send.at[target], mid.at[z], sems.at[0], sems.at[1], NC * target + c).start()
+        mid[z] = send[z]
+
+    def second_hop(mid, recv, sems):
+        wait_bytes(mid.at[pl.ds(0, NZ - 1)], sems.at[1])
+        for e in range(1, NC):
+            target = lax.rem(c + e, NC)
+            to_pool(mid.at[:, target], recv.at[:, c], sems.at[2], sems.at[3], NC * z + target).start()
+        for k in range(NZ):
+            recv[k, c] = mid[k, c]
+
+    def arrived(recv, sems):
+        wait_bytes(recv.at[pl.ds(0, NC - 1)], sems.at[3])
+
+    def put_rows(send, rows):
+        for peer in range(NP):
+            send[peer // NC, peer % NC] = rows[CAP * peer : CAP * (peer + 1), :]
+
+    def take_rows(recv):
+        for peer in range(NP):
+            rows_ref[CAP * peer : CAP * (peer + 1), :] = recv[peer // NC, peer % NC]
+
     p_copy = pltpu.make_async_copy(p_any, p_raw, sem_p)
     p_copy.start()
 
     barrier = pltpu.get_barrier_semaphore()
-
-    def greet(d, _):
-        pl.semaphore_signal(
-            barrier, inc=1, device_id=(lax.rem(me + d, NP), rep), device_id_type=MESH
-        )
-        return 0
-
-    lax.fori_loop(1, NP, greet, 0)
+    for e in range(1, NZ):
+        pl.semaphore_signal(barrier, inc=1, device_id=(along_z(e), rep), device_id_type=MESH)
+    for e in range(1, NC):
+        pl.semaphore_signal(barrier, inc=1, device_id=(in_plane(e), rep), device_id_type=MESH)
     for d in range(1, NR):
         pl.semaphore_signal(
             barrier, inc=1, device_id=(me, lax.rem(rep + d, NR)), device_id_type=MESH
@@ -107,28 +139,23 @@
         q_low[a] = (x * inv).astype(bf16)
 
     npair = GROUPS * NQ
-    mf = meta_ref[...].astype(f32)
-    cols = mf.shape[1]
-    lane_m = iota((NQ, cols), 1)
+    eye = iota((NQ, NQ), 0) == iota((NQ, NQ), 1)
+    own_f = own_ref[...].astype(f32)
     own_col = jnp.concatenate(
         [
-            jnp.sum(jnp.where(lane_m == g, mf, 0.0), axis=1, keepdims=True)
+            jnp.sum(jnp.where(eye, own_f[g : g + 1, :], 0.0), axis=1, keepdims=True)
             for g in range(GROUPS)
         ],
         axis=0,
     )
-    src_r, dst_c = iota((cols, 128), 0), iota((cols, 128), 1)
-    loc_w = jnp.concatenate(
-        [
-            dot(mf, hot((src_r == GROUPS + WIDTH * g + dst_c) & (dst_c < WIDTH)))
-            for g in range(GROUPS)
-        ],
-        axis=0,
-    )
-    mask_w = [
-        dot(mf, hot((src_r == GROUPS + GROUPS * WIDTH + WIDTH * g + dst_c) & (dst_c < WIDTH)))
-        for g in range(GROUPS)
-    ]
+    loc_f = dot_nt(hot(eye), loc_ref[...].astype(f32))
+    mask_f = mask_ref[...].astype(f32)
+    src_r, dst_c = iota((NQ, 128), 0), iota((NQ, 128), 1)
+    places = [hot((src_r == WIDTH * g + dst_c) & (dst_c < WIDTH)) for g in range(GROUPS)]
+    loc_w = jnp.concatenate([dot(loc_f, place) for place in places], axis=0)
+    mask_w = [dot(mask_f, place) for place in places]
+    pair_q = (iota((npair, 128), 0) % NQ).astype(f32)
+    loc_w = jnp.where(iota((npair, 128), 1) == WIDTH, pair_q, loc_w)
     ra, ca = iota((npair, npair), 0), iota((npair, npair), 1)
     own_row = jnp.sum(jnp.where(ra == ca, own_col, 0.0), axis=0, keepdims=True)
     same = own_col == own_row
@@ -138,45 +165,58 @@
     slot_row = CAP * own_row + rank_row
     st = hot(slot_col == iota((npair, SLOTS), 1).astype(f32))
     s_hot = hot(slot_row == iota((SLOTS, npair), 0).astype(f32))
-    qidx_row = jnp.sum(
-        st * (iota((npair, SLOTS), 0) % NQ).astype(f32), axis=0, keepdims=True
-    )
     slot_wide = jnp.sum(
         jnp.where(iota((npair, 128), 0) == iota((npair, 128), 1), slot_col, 0.0),
         axis=0, keepdims=True,
     )
-    tbla_v[0:8, :] = index(jnp.broadcast_to(qidx_row, (8, 128)), NQ)
-    tbla_v[8:16, :] = index(jnp.broadcast_to(slot_wide, (8, 128)), SLOTS)
+    tbla_v[...] = index(jnp.broadcast_to(slot_wide, (8, 128)), SLOTS)
     tbla_copy = pltpu.make_async_copy(tbla_v, tbla, sem_tbl)
     tbla_copy.start()
-    loc_slots = dot(s_hot, loc_w)
-    for peer in range(NP):
-        meta_send[peer] = loc_slots[CAP * peer : CAP * (peer + 1), :]
+    put_rows(m_a, dot(s_hot, loc_w))
     tbla_copy.wait()
-    pl.semaphore_wait(barrier, NP - 1 + NR - 1)
-
-    def send_meta(d, _):
-        peer = lax.rem(me + d, NP)
-        to_pool(meta_send.at[peer], meta_recv.at[me], m_ss, m_rs, peer).start()
-        return 0
-
-    lax.fori_loop(1, NP, send_meta, 0)
-    meta_recv[me] = meta_send[me]
-
-    def send_q(d, _):
-        peer = lax.rem(me + d, NP)
+    pl.semaphore_wait(barrier, NZ - 1 + NC - 1 + NR - 1)
+
+    first_hop(m_a, m_b, m_sem)
+
+    plus, minus = [q_low, plus1, plus2, plus3], [q_low, minus1, minus2, minus3]
+    half = NQ // 2
+
+    def pass_on(h):
+        if h < NZ // 2 - 1:
+            to_pool(plus[h], plus[h + 1], hop_s, plus_r.at[h], along_z(1)).start()
+            to_pool(minus[h], minus[h + 1], hop_s, minus_r.at[h], along_z(-1)).start()
+        else:
+            low, top = pl.ds(0, half), pl.ds(half, half)
+            to_pool(plus[h].at[low], far.at[low], hop_s, plus_r.at[h], along_z(1)).start()
+            to_pool(minus[h].at[top], far.at[top], hop_s, minus_r.at[h], along_z(-1)).start()
+
+    pass_on(0)
+
+    second_hop(m_b, m_c, m_sem)
+    take_rows(m_b)
+    r_i, c_i = iota((128, 128), 0), iota((128, 128), 1)
+    picked = jnp.sum(
+        jnp.where(r_i == c_i, rows_ref[:, WIDTH : WIDTH + 1], 0.0), axis=0, keepdims=True
+    )
+    tblm_v[...] = index(jnp.broadcast_to(picked, (8, 128)), NQ)
+    tblm_copy = pltpu.make_async_copy(tblm_v, tblm, sem_tbl)
+    tblm_copy.start()
+    tblm_copy.wait()
+
+    def deliver(block, source):
+        for e in range(1, NC):
+            target = lax.rem(c + e, NC)
+            row = CAP * (NC * source + target)
+            for k in range(CAP):
+                q_send[row + k] = block[tblm[0, row + k]]
+            to_pool(
+                q_send.at[pl.ds(row, CAP)],
+                q_recv.at[pl.ds(CAP * (NC * source + c), CAP)],
+                q_ss, q_rs, NC * z + target,
+            ).start()
+        row = CAP * (NC * source + c)
         for k in range(CAP):
-            q_send[CAP * peer + k] = q_low[tbla[0, CAP * peer + k]]
-        to_pool(
-            q_send.at[pl.ds(CAP * peer, CAP)], q_recv.at[pl.ds(CAP * me, CAP)], q_ss, q_rs, peer
-        ).start()
-        return 0
-
-    lax.fori_loop(1, NP, send_q, 0)
-    for k in range(CAP):
-        q_recv[CAP * me + k] = q_low[tbla[0, CAP * me + k]]
-
-    p_copy.wait()
+            q_recv[row + k] = block[tblm[0, row + k]]
 
     def norm_passage(p, _):
         x = p_raw[p].astype(f32)
@@ -184,13 +224,21 @@
         p_low[p] = (x * inv).astype(bf16)
         return 0
 
-    lax.fori_loop(0, NPASS, norm_passage, 0, unroll=2)
-
-    wait_bytes(meta_recv.at[pl.ds(0, NP - 1)], m_rs)
-    for peer in range(NP):
-        rows_ref[CAP * peer : CAP * (peer + 1), :] = meta_recv[peer]
+    deliver(q_low, z)
+    p_copy.wait()
+    for h in range(1, NZ // 2):
+        wait_bytes(plus[h], plus_r.at[h - 1])
+        wait_bytes(minus[h], minus_r.at[h - 1])
+        pass_on(h)
+        deliver(plus[h], lax.rem(z + NZ - h, NZ))
+        deliver(minus[h], lax.rem(z + h, NZ))
+        part = NPASS // (NZ // 2)
+        lax.fori_loop(part * (h - 1), part * h, norm_passage, 0, unroll=2)
+    lax.fori_loop(NPASS - part, NPASS, norm_passage, 0, unroll=2)
+
+    arrived(m_c, m_sem)
+    take_rows(m_c)
     loc_r = rows_ref[...]
-    r_i, c_i = iota((128, 128), 0), iota((128, 128), 1)
     pc, jc, pr, jr = c_i % NPASS, c_i // NPASS, r_i % NPASS, r_i // NPASS
     one_hot = hot(dot(loc_r, hot((r_i == jc) & (r_i < WIDTH))) == pc.astype(f32))
     before = dot(hot(c_i < r_i), one_hot)
@@ -233,7 +281,10 @@
     tblb_copy.start()
     tblb_copy.wait()
 
-    wait_bytes(q_recv.at[pl.ds(0, CAP * (NP - 1))], q_rs)
+    wait_bytes(far.at[pl.ds(0, half)], plus_r.at[NZ // 2 - 1])
+    wait_bytes(far.at[pl.ds(half, half)], minus_r.at[NZ // 2 - 1])
+    deliver(far, lax.rem(z + NZ // 2, NZ))
+    wait_bytes(q_recv.at[pl.ds(0, CAP * NZ * (NC - 1))], q_rs)
     ones = jnp.ones((PT, DIM), bf16)
     lane8 = iota((8, 128), 1)
 
@@ -271,19 +322,11 @@
             jnp.where(rest_c[:, j : j + 1] == lane_r, picked, 0.0), axis=1, keepdims=True
         )
         sc = jnp.where(lane_s == j, col, sc)
-    for peer in range(NP):
-        sc_send[peer] = sc[CAP * peer : CAP * (peer + 1), :]
-
-    def send_sc(d, _):
-        peer = lax.rem(me + d, NP)
-        to_pool(sc_send.at[peer], sc_recv.at[me], s_ss, s_rs, peer).start()
-        return 0
-
-    lax.fori_loop(1, NP, send_sc, 0)
-    sc_recv[me] = sc_send[me]
-    wait_bytes(sc_recv.at[pl.ds(0, NP - 1)], s_rs)
-    for peer in range(NP):
-        rows_ref[CAP * peer : CAP * (peer + 1), :] = sc_recv[peer]
+    put_rows(s_a, sc)
+    first_hop(s_a, s_b, s_sem)
+    second_hop(s_b, s_c, s_sem)
+    arrived(s_c, s_sem)
+    take_rows(s_c)
 
     own_scores = hdot(st, rows_ref[...])
     lane_q = iota((NQ, 128), 1)
@@ -303,19 +346,11 @@
     dscore = [LOSS_SCALE * (e / denom) for e in exps]
     dscore[0] = dscore[0] - jnp.where(lane_q == 0, LOSS_SCALE, 0.0)
     w_slots = hdot(s_hot, jnp.concatenate(dscore, axis=0))
-    for peer in range(NP):
-        w_send[peer] = w_slots[CAP * peer : CAP * (peer + 1), :]
-
-    def send_w(d, _):
-        peer = lax.rem(me + d, NP)
-        to_pool(w_send.at[peer], w_recv.at[me], w_ss, w_rs, peer).start()
-        return 0
-
-    lax.fori_loop(1, NP, send_w, 0)
-    w_recv[me] = w_send[me]
-    wait_bytes(w_recv.at[pl.ds(0, NP - 1)], w_rs)
-    for peer in range(NP):
-        rows_ref[CAP * peer : CAP * (peer + 1), :] = w_recv[peer]
+    put_rows(w_a, w_slots)
+    first_hop(w_a, w_b, w_sem)
+    second_hop(w_b, w_c, w_sem)
+    arrived(w_c, w_sem)
+    take_rows(w_c)
 
     w_rows = hdot_nt(hot(iota((8, 128), 0) == iota((8, 128), 1)), rows_ref[...])
     w_tile = jnp.zeros((8, 128), f32)
@@ -404,7 +439,7 @@
         unit = x * inv
         up = jnp.zeros((QT, DIM), f32)
         for g in range(GROUPS):
-            up = up + ret_recv[tbla[8, NQ * g + a]].astype(f32)
+            up = up + ret_recv[tbla[0, NQ * g + a]].astype(f32)
         gq_ref[a] = inv * (up - unit * jnp.sum(unit * up, axis=-1, keepdims=True))
         return 0
 
@@ -425,37 +460,55 @@
 
     lax.fori_loop(0, NPASS, finish_passage, 0, unroll=4)
 
-    wait_bytes(meta_send.at[pl.ds(0, NP - 1)], m_ss)
-    wait_bytes(q_send.at[pl.ds(0, CAP * (NP - 1))], q_ss)
-    wait_bytes(sc_send.at[pl.ds(0, NP - 1)], s_ss)
-    wait_bytes(w_send.at[pl.ds(0, NP - 1)], w_ss)
+    for send, sems in ((m_a, m_sem), (s_a, s_sem), (w_a, w_sem)):
+        wait_bytes(send.at[pl.ds(0, NZ - 1)], sems.at[0])
+        wait_bytes(send.at[pl.ds(0, NC - 1)], sems.at[2])
+    wait_bytes(q_send.at[pl.ds(0, NQ * (NZ - 1))], hop_s)
+    wait_bytes(q_send.at[pl.ds(0, CAP * NZ * (NC - 1))], q_ss)
     wait_bytes(ret_send.at[pl.ds(0, CAP * (NP - 1))], r_ss)
     wait_bytes(rs_recv, x_ss)
 
 
+def leave(loss_in, gq_in, gp_in, loss_out, gq_out, gp_out, sems):
+    copies = [
+        pltpu.make_async_copy(src, dst, sems.at[i])
+        for i, (src, dst) in enumerate(
+            ((gp_in, gp_out), (gq_in, gq_out), (loss_in, loss_out))
+        )
+    ]
+    for copy in copies:
+        copy.start()
+    for copy in copies:
+        copy.wait()
+
+
 def per_device(query_vecs, passage_vecs, owner_ids, local_ids, cand_mask):
-    meta = jnp.concatenate(
-        [owner_ids, local_ids.reshape(NQ, GROUPS * WIDTH), cand_mask], axis=1
-    )
     vmem = pl.BlockSpec(memory_space=pltpu.VMEM)
-    rows = pltpu.VMEM((NP, CAP, 128), f32)
+    anywhere = pl.BlockSpec(memory_space=pl.ANY)
+    rows = pltpu.VMEM((NZ, NC, CAP, 128), f32)
+    block = pltpu.VMEM((NQ, QT, DIM), bf16)
     dma = pltpu.SemaphoreType.DMA
-    loss, grad_query, grad_passage = pl.pallas_call(
+    outs = (
+        jax.ShapeDtypeStruct((1, NQ), f32),
+        jax.ShapeDtypeStruct((NQ, QT, DIM), f32),
+        jax.ShapeDtypeStruct((NPASS, SHARE, DIM), f32),
+    )
+    results = pl.pallas_call(
         kernel,
-        out_shape=(
-            jax.ShapeDtypeStruct((1, NQ), f32),
-            jax.ShapeDtypeStruct((NQ, QT, DIM), f32),
-            jax.ShapeDtypeStruct((NPASS, SHARE, DIM), f32),
-        ),
-        in_specs=[vmem, pl.BlockSpec(memory_space=pl.ANY), vmem],
+        out_shape=outs,
+        in_specs=[vmem, anywhere, vmem, vmem, vmem],
         out_specs=[vmem, vmem, vmem],
         scratch_shapes=[
             pltpu.VMEM((NPASS, PT, DIM), bf16),
             pltpu.VMEM((NPASS, PT, DIM), bf16),
-            pltpu.VMEM((NQ, QT, DIM), bf16),
+        ]
+        + [block] * 8
+        + [
             pltpu.VMEM((SLOTS, QT, DIM), bf16),
             pltpu.VMEM((SLOTS, QT, DIM), bf16),
-            rows, rows, rows, rows, rows, rows,
+        ]
+        + [rows] * 9
+        + [
             pltpu.VMEM((SLOTS, 128), f32),
             pltpu.VMEM((WIDTH, 128, 128), f32),
             pltpu.VMEM((NTILES, TILE * QT, PT), bf16),
@@ -465,18 +518,35 @@
             pltpu.VMEM((SLOTS, QT, DIM), bf16),
             pltpu.VMEM((NR, NPASS, SHARE, DIM), bf16),
             pltpu.VMEM((NR - 1, NPASS, SHARE, DIM), bf16),
-            pltpu.VMEM((16, 128), i32),
+            pltpu.VMEM((8, 128), i32),
+            pltpu.VMEM((8, 128), i32),
             pltpu.VMEM((40, 128), i32),
             pltpu.VMEM((8, 128), f32),
-            pltpu.SMEM((16, 128), i32),
+            pltpu.SMEM((8, 128), i32),
+            pltpu.SMEM((8, 128), i32),
             pltpu.SMEM((40, 128), i32),
             pltpu.SMEM((8, 128), f32),
         ]
-        + [dma(())] * 14,
+        + [dma(()), dma(()), dma(()), dma((NZ // 2,)), dma((NZ // 2,)), dma(()), dma(())]
+        + [dma((4,))] * 3
+        + [dma(())] * 4,
         compiler_params=pltpu.CompilerParams(
             collective_id=0, has_side_effects=True, vmem_limit_bytes=62 * 1024 * 1024
         ),
-    )(query_vecs, passage_vecs, meta)
+    )(
+        query_vecs,
+        passage_vecs,
+        owner_ids.T,
+        local_ids.transpose(1, 2, 0).reshape(GROUPS * WIDTH, NQ),
+        cand_mask,
+    )
+    loss, grad_query, grad_passage = pl.pallas_call(
+        leave,
+        out_shape=outs,
+        in_specs=[anywhere] * 3,
+        out_specs=[anywhere] * 3,
+        scratch_shapes=[dma((3,))],
+    )(*results)
     return (loss.reshape(NQ), grad_query, grad_passage)
 
 

time: 106 us -> 138 us (1.30)
  Pallas kernels: 96.9 us -> 137 us
  local copies, waits for them, and re-layouts: 6.62 us -> 0 us
    pallas_call x1 -> x2, Pallas kernels: 96.9 us -> 137 us  [the longest x1 96.6 us: per_device(): pl.pallas_call(kernel, out_shape=outs, in_specs=[vmem, anywhere, vmem, vm...]
    unnamed x4 -> x0, local copies, waits for them, and re-layouts: 5.86 us -> none
where the time goes in v3:
time: 138 us
  Pallas kernels  137 us (99%)
    pallas_call x1, Pallas kernels, per_device(): pl.pallas_call(kernel, out_shape=outs, in_specs=[vmem, anywhere, vmem, vm...  96.6 us
    pallas_call x1, Pallas kernels, per_device(): pl.pallas_call(leave, out_shape=outs, in_specs=[anywhere] * 3, out_specs=...  40.9 us

profile of v3, /device:TPU:1, one launch (start us, length us, event | category | flops | bytes accessed | tf_op | source)
XLA Modules:
  0.0 138.1 jit_solution(17757732600761922445)
XLA Ops:
  0.6 96.6 %shard_map.76 = (f32[1,16]{1,0:T(1,128)}, f32[16,32,128]{2,1,0:T(8,128)}, f32[32,64,128]{2,1,0:T(8,128)}) custom-call(bf16[16,32,128]{2,1,0:T(8,128)(2,1)} %q_ref.1, bf16[32,256,128]{2,1,0:T(8,128)(2,1)} %p_any.1, s32[4,16]{1,0:T(4,128)} %bitcast.6, s32[16,16]{1,0:T(8,128)} %bitcast.5, s32[16,16]{1,0:T(8,128)} %mask_ref.1), custom_call_target="tpu_custom_call" | custom-call | tf_op jit(solution)/shard_map/pallas_call | solution.py:496
  97.3 40.9 %shard_map.77 = (f32[1,16]{1,0:T(1,128)}, f32[16,32,128]{2,1,0:T(8,128)}, f32[32,64,128]{2,1,0:T(8,128)}) custom-call(f32[1,16]{1,0:T(1,128)} %get-tuple-element.9.loss_in, f32[16,32,128]{2,1,0:T(8,128)} %get-tuple-element.10.gq_in, f32[32,64,128]{2,1,0:T(8,128)} %get-tuple-element.11.gp_in), custom_call_target="tpu_custom_call" | custom-call | tf_op jit(solution)/shard_map/pallas_call | solution.py:543

commit v4 on v3

--- a/solution.py
+++ b/solution.py
@@ -18,6 +18,7 @@
 NR = 4
 NZ = 8
 NC = NP // NZ
+PIECES = 4
 CAP = 2
 NQ = 16
 QT = 32
@@ -69,12 +70,12 @@
 
 def kernel(
     q_ref, p_any, own_ref, loc_ref, mask_ref,
-    loss_ref, gq_ref, gp_ref,
+    loss_ref, uq_ref, up_ref,
     p_raw, p_low, q_low, plus1, plus2, plus3, minus1, minus2, minus3, far, q_send, q_recv,
     m_a, m_b, m_c, s_a, s_b, s_c, w_a, w_b, w_c,
-    rows_ref, rhs_ref, soft_ref, a_ref, qn_ref, ret_send, ret_recv, rs_send, rs_recv,
+    rows_ref, rhs_ref, soft_ref, a_ref, qn_ref, ret_send, ret_recv, rs_send, rs_recv, via_plus, via_minus, sum_plus, sum_minus,
     tbla_v, tblm_v, tblb_v, wt_v, tbla, tblm, tblb, wt,
-    sem_p, sem_tbl, hop_s, plus_r, minus_r, q_ss, q_rs, m_sem, s_sem, w_sem, r_ss, r_rs, x_ss, x_rs,
+    sem_p, sem_tbl, hop_s, plus_r, minus_r, q_ss, q_rs, m_sem, s_sem, w_sem, r_ss, r_rs, x_ss, x_rs, v_rs,
 ):
     me = lax.axis_index("pool")
     rep = lax.axis_index("rep")
@@ -178,19 +179,31 @@
 
     first_hop(m_a, m_b, m_sem)
 
-    plus, minus = [q_low, plus1, plus2, plus3], [q_low, minus1, minus2, minus3]
-    half = NQ // 2
-
-    def pass_on(h):
-        if h < NZ // 2 - 1:
-            to_pool(plus[h], plus[h + 1], hop_s, plus_r.at[h], along_z(1)).start()
-            to_pool(minus[h], minus[h + 1], hop_s, minus_r.at[h], along_z(-1)).start()
-        else:
-            low, top = pl.ds(0, half), pl.ds(half, half)
-            to_pool(plus[h].at[low], far.at[low], hop_s, plus_r.at[h], along_z(1)).start()
-            to_pool(minus[h].at[top], far.at[top], hop_s, minus_r.at[h], along_z(-1)).start()
-
-    pass_on(0)
+    plus = [q_low, plus1, plus2, plus3, far]
+    minus = [q_low, minus1, minus2, minus3, far]
+    last_hop = NZ // 2 - 1
+    piece = NQ // PIECES
+
+    def pass_on(h, k):
+        rows = pl.ds(piece * k, piece)
+        if h < last_hop or 2 * k < PIECES:
+            to_pool(
+                plus[h].at[rows], plus[h + 1].at[rows], hop_s, plus_r.at[PIECES * h + k], along_z(1)
+            ).start()
+        if h < last_hop or 2 * k >= PIECES:
+            to_pool(
+                minus[h].at[rows], minus[h + 1].at[rows], hop_s, minus_r.at[PIECES * h + k], along_z(-1)
+            ).start()
+
+    def relay(h):
+        for k in range(PIECES):
+            rows = pl.ds(piece * k, piece)
+            wait_bytes(plus[h].at[rows], plus_r.at[PIECES * (h - 1) + k])
+            wait_bytes(minus[h].at[rows], minus_r.at[PIECES * (h - 1) + k])
+            pass_on(h, k)
+
+    for k in range(PIECES):
+        pass_on(0, k)
 
     second_hop(m_b, m_c, m_sem)
     take_rows(m_b)
@@ -201,7 +214,6 @@
     tblm_v[...] = index(jnp.broadcast_to(picked, (8, 128)), NQ)
     tblm_copy = pltpu.make_async_copy(tblm_v, tblm, sem_tbl)
     tblm_copy.start()
-    tblm_copy.wait()
 
     def deliver(block, source):
         for e in range(1, NC):
@@ -218,23 +230,31 @@
         for k in range(CAP):
             q_recv[row + k] = block[tblm[0, row + k]]
 
+    def deliver_both(h):
+        deliver(plus[h], lax.rem(z + NZ - h, NZ))
+        deliver(minus[h], lax.rem(z + h, NZ))
+
     def norm_passage(p, _):
         x = p_raw[p].astype(f32)
         inv = lax.rsqrt(jnp.sum(x * x, axis=-1, keepdims=True) + EPSILON)
         p_low[p] = (x * inv).astype(bf16)
         return 0
 
+    relay(1)
+    tblm_copy.wait()
     deliver(q_low, z)
+    relay(2)
+    deliver_both(1)
+    relay(3)
+    deliver_both(2)
+    deliver_both(3)
     p_copy.wait()
-    for h in range(1, NZ // 2):
-        wait_bytes(plus[h], plus_r.at[h - 1])
-        wait_bytes(minus[h], minus_r.at[h - 1])
-        pass_on(h)
-        deliver(plus[h], lax.rem(z + NZ - h, NZ))
-        deliver(minus[h], lax.rem(z + h, NZ))
-        part = NPASS // (NZ // 2)
-        lax.fori_loop(part * (h - 1), part * h, norm_passage, 0, unroll=2)
-    lax.fori_loop(NPASS - part, NPASS, norm_passage, 0, unroll=2)
+    lax.fori_loop(0, NPASS // 2, norm_passage, 0, unroll=2)
+    for k in range(PIECES):
+        rows = pl.ds(piece * k, piece)
+        arrival = plus_r if 2 * k < PIECES else minus_r
+        wait_bytes(far.at[rows], arrival.at[PIECES * last_hop + k])
+    deliver(far, lax.rem(z + NZ // 2, NZ))
 
     arrived(m_c, m_sem)
     take_rows(m_c)
@@ -279,11 +299,9 @@
     tblb_v[32:40, :] = index(tiles, 2)
     tblb_copy = pltpu.make_async_copy(tblb_v, tblb, sem_tbl)
     tblb_copy.start()
+    lax.fori_loop(NPASS // 2, NPASS, norm_passage, 0, unroll=2)
     tblb_copy.wait()
 
-    wait_bytes(far.at[pl.ds(0, half)], plus_r.at[NZ // 2 - 1])
-    wait_bytes(far.at[pl.ds(half, half)], minus_r.at[NZ // 2 - 1])
-    deliver(far, lax.rem(z + NZ // 2, NZ))
     wait_bytes(q_recv.at[pl.ds(0, CAP * NZ * (NC - 1))], q_rs)
     ones = jnp.ones((PT, DIM), bf16)
     lane8 = iota((8, 128), 1)
@@ -403,6 +421,13 @@
 
     lax.fori_loop(0, NTILES, passage_tile, jnp.zeros((PT, DIM), f32), unroll=UNROLL)
 
+    after, opposite, before_me = (lax.rem(rep + d, NR) for d in (1, 2, 3))
+
+    def to_rep(src, dst, rs, target):
+        pltpu.make_async_remote_copy(
+            src_ref=src, dst_ref=dst, send_sem=x_ss, recv_sem=rs, device_id=(me, target), device_id_type=MESH
+        ).start()
+
     for chunk in range(NPASS // RS_CHUNK):
 
         def cut_passage(i, _):
@@ -420,45 +445,55 @@
 
         lax.fori_loop(0, RS_CHUNK, cut_passage, 0, unroll=RS_CHUNK)
         rows = pl.ds(chunk * RS_CHUNK, RS_CHUNK)
-        for d in range(1, NR):
-            target = lax.rem(rep + d, NR)
-            pltpu.make_async_remote_copy(
-                src_ref=rs_send.at[target, rows],
-                dst_ref=rs_recv.at[d - 1, rows],
-                send_sem=x_ss,
-                recv_sem=x_rs,
-                device_id=(me, target),
-                device_id_type=MESH,
-            ).start()
+        if 2 * chunk * RS_CHUNK < NPASS:
+            to_rep(rs_send.at[opposite, rows], via_plus.at[rows], v_rs.at[0], after)
+            to_rep(rs_send.at[before_me, rows], rs_recv.at[1, rows], x_rs, before_me)
+        else:
+            back = pl.ds(chunk * RS_CHUNK - NPASS // 2, RS_CHUNK)
+            to_rep(rs_send.at[opposite, rows], via_minus.at[back], v_rs.at[1], before_me)
+            to_rep(rs_send.at[after, rows], rs_recv.at[0, rows], x_rs, after)
+
+    low, top = pl.ds(0, NPASS // 2), pl.ds(NPASS // 2, NPASS // 2)
+    wait_bytes(via_plus, v_rs.at[0])
+
+    def add_plus(i, _):
+        sum_plus[i] = (rs_send[after, i].astype(f32) + via_plus[i].astype(f32)).astype(bf16)
+        return 0
+
+    lax.fori_loop(0, NPASS // 2, add_plus, 0, unroll=4)
+    to_rep(sum_plus, rs_recv.at[0, low], x_rs, after)
+    wait_bytes(via_minus, v_rs.at[1])
+
+    def add_minus(i, _):
+        sum_minus[i] = (
+            rs_send[before_me, NPASS // 2 + i].astype(f32) + via_minus[i].astype(f32)
+        ).astype(bf16)
+        return 0
+
+    lax.fori_loop(0, NPASS // 2, add_minus, 0, unroll=4)
+    to_rep(sum_minus, rs_recv.at[1, top], x_rs, before_me)
 
     wait_bytes(ret_recv.at[pl.ds(0, CAP * (NP - 1))], r_rs)
 
-    def finish_query(a, _):
-        x = q_ref[a].astype(f32)
-        inv = lax.rsqrt(jnp.sum(x * x, axis=-1, keepdims=True) + EPSILON)
-        unit = x * inv
+    def sum_query(a, _):
         up = jnp.zeros((QT, DIM), f32)
         for g in range(GROUPS):
             up = up + ret_recv[tbla[0, NQ * g + a]].astype(f32)
-        gq_ref[a] = inv * (up - unit * jnp.sum(unit * up, axis=-1, keepdims=True))
+        uq_ref[a] = up
         return 0
 
-    lax.fori_loop(0, NQ, finish_query, 0, unroll=4)
+    lax.fori_loop(0, NQ, sum_query, 0, unroll=4)
 
     wait_bytes(rs_recv, x_rs)
-    start = pl.multiple_of(rep * SHARE, SHARE)
-
-    def finish_passage(p, _):
-        x = p_raw[p, pl.ds(start, SHARE), :].astype(f32)
-        inv = lax.rsqrt(jnp.sum(x * x, axis=-1, keepdims=True) + EPSILON)
-        unit = x * inv
+
+    def sum_passage(p, _):
         up = rs_send[rep, p].astype(f32)
-        for d in range(NR - 1):
+        for d in range(2):
             up = up + rs_recv[d, p].astype(f32)
-        gp_ref[p] = inv * (up - unit * jnp.sum(unit * up, axis=-1, keepdims=True))
+        up_ref[p] = up
         return 0
 
-    lax.fori_loop(0, NPASS, finish_passage, 0, unroll=4)
+    lax.fori_loop(0, NPASS, sum_passage, 0, unroll=4)
 
     for send, sems in ((m_a, m_sem), (s_a, s_sem), (w_a, w_sem)):
         wait_bytes(send.at[pl.ds(0, NZ - 1)], sems.at[0])
@@ -466,20 +501,31 @@
     wait_bytes(q_send.at[pl.ds(0, NQ * (NZ - 1))], hop_s)
     wait_bytes(q_send.at[pl.ds(0, CAP * NZ * (NC - 1))], q_ss)
     wait_bytes(ret_send.at[pl.ds(0, CAP * (NP - 1))], r_ss)
-    wait_bytes(rs_recv, x_ss)
-
-
-def leave(loss_in, gq_in, gp_in, loss_out, gq_out, gp_out, sems):
-    copies = [
-        pltpu.make_async_copy(src, dst, sems.at[i])
-        for i, (src, dst) in enumerate(
-            ((gp_in, gp_out), (gq_in, gq_out), (loss_in, loss_out))
-        )
-    ]
-    for copy in copies:
+    wait_bytes(rs_send.at[pl.ds(0, NR - 1)], x_ss)
+
+
+def unit_backward(x, up):
+    x = x.astype(f32)
+    inv = lax.rsqrt(jnp.sum(x * x, axis=-1, keepdims=True) + EPSILON)
+    unit = x * inv
+    return inv * (up - unit * jnp.sum(unit * up, axis=-1, keepdims=True))
+
+
+def finish(loss_in, q_ref, uq_ref, p_any, up_ref, loss_ref, gq_ref, gp_ref, p_share, sem):
+    step = pl.program_id(0)
+
+    @pl.when(step == 0)
+    def _():
+        start = pl.multiple_of(lax.axis_index("rep") * SHARE, SHARE)
+        copy = pltpu.make_async_copy(p_any.at[:, pl.ds(start, SHARE)], p_share, sem)
         copy.start()
-    for copy in copies:
+        loss_ref[...] = loss_in[...]
+        for a in range(NQ):
+            gq_ref[a] = unit_backward(q_ref[a], uq_ref[a])
         copy.wait()
+
+    for i in range(RS_CHUNK):
+        gp_ref[i] = unit_backward(p_share[step * RS_CHUNK + i], up_ref[i])
 
 
 def per_device(query_vecs, passage_vecs, owner_ids, local_ids, cand_mask):
@@ -493,7 +539,7 @@
         jax.ShapeDtypeStruct((NQ, QT, DIM), f32),
         jax.ShapeDtypeStruct((NPASS, SHARE, DIM), f32),
     )
-    results = pl.pallas_call(
+    loss, up_query, up_passage = pl.pallas_call(
         kernel,
         out_shape=outs,
         in_specs=[vmem, anywhere, vmem, vmem, vmem],
@@ -517,7 +563,10 @@
             pltpu.VMEM((SLOTS, QT, DIM), bf16),
             pltpu.VMEM((SLOTS, QT, DIM), bf16),
             pltpu.VMEM((NR, NPASS, SHARE, DIM), bf16),
-            pltpu.VMEM((NR - 1, NPASS, SHARE, DIM), bf16),
+            pltpu.VMEM((2, NPASS, SHARE, DIM), bf16),
+        ]
+        + [pltpu.VMEM((NPASS // 2, SHARE, DIM), bf16)] * 4
+        + [
             pltpu.VMEM((8, 128), i32),
             pltpu.VMEM((8, 128), i32),
             pltpu.VMEM((40, 128), i32),
@@ -527,9 +576,10 @@
             pltpu.SMEM((40, 128), i32),
             pltpu.SMEM((8, 128), f32),
         ]
-        + [dma(()), dma(()), dma(()), dma((NZ // 2,)), dma((NZ // 2,)), dma(()), dma(())]
+        + [dma(()), dma(()), dma(()), dma((PIECES * NZ // 2,)), dma((PIECES * NZ // 2,)), dma(()), dma(())]
         + [dma((4,))] * 3
-        + [dma(())] * 4,
+        + [dma(())] * 4
+        + [dma((2,))],
         compiler_params=pltpu.CompilerParams(
             collective_id=0, has_side_effects=True, vmem_limit_bytes=62 * 1024 * 1024
         ),
@@ -540,13 +590,16 @@
         local_ids.transpose(1, 2, 0).reshape(GROUPS * WIDTH, NQ),
         cand_mask,
     )
+    whole = lambda shape: pl.BlockSpec(shape, lambda i: (0,) * len(shape))
+    part = pl.BlockSpec((RS_CHUNK, SHARE, DIM), lambda i: (i, 0, 0))
     loss, grad_query, grad_passage = pl.pallas_call(
-        leave,
+        finish,
+        grid=(NPASS // RS_CHUNK,),
         out_shape=outs,
-        in_specs=[anywhere] * 3,
-        out_specs=[anywhere] * 3,
-        scratch_shapes=[dma((3,))],
-    )(*results)
+        in_specs=[whole((1, NQ)), whole((NQ, QT, DIM)), whole((NQ, QT, DIM)), anywhere, part],
+        out_specs=[whole((1, NQ)), whole((NQ, QT, DIM)), part],
+        scratch_shapes=[pltpu.VMEM((NPASS, SHARE, DIM), bf16), dma(())],
+    )(loss, query_vecs, up_query, passage_vecs, up_passage)
     return (loss.reshape(NQ), grad_query, grad_passage)
 
 

time: 138 us -> 93.5 us (0.68)
  Pallas kernels: 137 us -> 92.7 us
    pallas_call x1, Pallas kernels: 40.9 us -> 5.03 us  [per_device(): pl.pallas_call(finish, grid=(NPASS // RS_CHUNK,), out_shape=outs, in_spec...]
    pallas_call x1, Pallas kernels: 96.6 us -> 87.7 us  [per_device(): pl.pallas_call(kernel, out_shape=outs, in_specs=[vmem, anywhere, vmem, vm...]
where the time goes in v4:
time: 93.5 us; the launch traced here: 93.3 us
  Pallas kernels  92.7 us (99%)
    pallas_call x1, Pallas kernels, per_device(): pl.pallas_call(kernel, out_shape=outs, in_specs=[vmem, anywhere, vmem, vm...  87.7 us
    pallas_call x1, Pallas kernels, per_device(): pl.pallas_call(finish, grid=(NPASS // RS_CHUNK,), out_shape=outs, in_spec...  5.03 us

profile of v4, /device:TPU:1, one launch (start us, length us, event | category | flops | bytes accessed | tf_op | source)
XLA Modules:
  0.0 93.3 jit_solution(14953186629359328945)
XLA Ops:
  0.6 87.7 %shard_map.76 = (f32[1,16]{1,0:T(1,128)}, f32[16,32,128]{2,1,0:T(8,128)}, f32[32,64,128]{2,1,0:T(8,128)}) custom-call(bf16[16,32,128]{2,1,0:T(8,128)(2,1)} %q_ref.3, bf16[32,256,128]{2,1,0:T(8,128)(2,1)} %p_any.3, s32[4,16]{1,0:T(4,128)} %bitcast.6, s32[16,16]{1,0:T(8,128)} %bitcast.5, s32[16,16]{1,0:T(8,128)} %mask_ref.1), custom_call_target="tpu_custom_call" | custom-call | tf_op jit(solution)/shard_map/pallas_call | solution.py:542
  88.3 5.0 %shard_map.77 = (f32[1,16]{1,0:T(1,128)}, f32[16,32,128]{2,1,0:T(8,128)}, f32[32,64,128]{2,1,0:T(8,128)}) custom-call(f32[1,16]{1,0:T(1,128)} %get-tuple-element.9.loss_in, bf16[16,32,128]{2,1,0:T(8,128)(2,1)} %q_ref.3, f32[16,32,128]{2,1,0:T(8,128)} %get-tuple-element.10.uq_ref, bf16[32,256,128]{2,1,0:T(8,128)(2,1)} %p_any.3, ...), custom_call_target="tpu_custom_call" | custom-call | tf_op jit(solution)/shard_map/pallas_call | solution.py:595

commit v5 on v4

--- a/solution.py
+++ b/solution.py
@@ -17,6 +17,7 @@
 NP = 64
 NR = 4
 NZ = 8
+NX = 4
 NC = NP // NZ
 PIECES = 4
 CAP = 2
@@ -73,14 +74,15 @@
     loss_ref, uq_ref, up_ref,
     p_raw, p_low, q_low, plus1, plus2, plus3, minus1, minus2, minus3, far, q_send, q_recv,
     m_a, m_b, m_c, s_a, s_b, s_c, w_a, w_b, w_c,
-    rows_ref, rhs_ref, soft_ref, a_ref, qn_ref, ret_send, ret_recv, rs_send, rs_recv, via_plus, via_minus, sum_plus, sum_minus,
+    rows_ref, rhs_ref, soft_ref, a_ref, qn_ref, ret_send, ret_recv, rs_send, rs_recv, via_plus, via_minus, sum_plus, sum_minus, q_via, ret_via,
     tbla_v, tblm_v, tblb_v, wt_v, tbla, tblm, tblb, wt,
-    sem_p, sem_tbl, hop_s, plus_r, minus_r, q_ss, q_rs, m_sem, s_sem, w_sem, r_ss, r_rs, x_ss, x_rs, v_rs,
+    sem_p, sem_tbl, hop_s, plus_r, minus_r, q_ss, q_rs, m_sem, s_sem, w_sem, r_ss, r_rs, x_ss, x_rs, v_rs, q_vr, ret_vs, ret_vr,
 ):
     me = lax.axis_index("pool")
     rep = lax.axis_index("rep")
     z = lax.div(me, NC)
     c = lax.rem(me, NC)
+    col, core = lax.div(c, 2), lax.rem(c, 2)
 
     def wait_bytes(ref, sem):
         pltpu.make_async_copy(ref, ref, sem).wait()
@@ -215,24 +217,51 @@
     tblm_copy = pltpu.make_async_copy(tblm_v, tblm, sem_tbl)
     tblm_copy.start()
 
-    def deliver(block, source):
-        for e in range(1, NC):
-            target = lax.rem(c + e, NC)
+    def chip(dx):
+        return 2 * lax.rem(col + NX + dx, NX)
+
+    def deliver(block, source, via=None):
+        def fill(target):
             row = CAP * (NC * source + target)
             for k in range(CAP):
                 q_send[row + k] = block[tblm[0, row + k]]
-            to_pool(
-                q_send.at[pl.ds(row, CAP)],
-                q_recv.at[pl.ds(CAP * (NC * source + c), CAP)],
-                q_ss, q_rs, NC * z + target,
-            ).start()
+            return row
+
+        for dx in (2, 1, 3, 0):
+            if dx == 2 and via is not None:
+                row = fill(chip(2))
+                fill(chip(2) + 1)
+                to_pool(
+                    q_send.at[pl.ds(row, 2 * CAP)], q_via.at[via], q_ss, q_vr.at[via],
+                    NC * z + chip(-1) + core,
+                ).start()
+                continue
+            for dc in range(2):
+                if dx == 0 and dc == 0:
+                    continue
+                target = chip(dx) + lax.rem(core + dc, 2)
+                row = fill(target)
+                to_pool(
+                    q_send.at[pl.ds(row, CAP)],
+                    q_recv.at[pl.ds(CAP * (NC * source + c), CAP)],
+                    q_ss, q_rs, NC * z + target,
+                ).start()
         row = CAP * (NC * source + c)
         for k in range(CAP):
             q_recv[row + k] = block[tblm[0, row + k]]
 
-    def deliver_both(h):
-        deliver(plus[h], lax.rem(z + NZ - h, NZ))
-        deliver(minus[h], lax.rem(z + h, NZ))
+    def forward_via(via, source):
+        wait_bytes(q_via.at[via], q_vr.at[via])
+        sender = chip(1) + core
+        for k in range(2):
+            to_pool(
+                q_via.at[via, pl.ds(CAP * k, CAP)],
+                q_recv.at[pl.ds(CAP * (NC * source + sender), CAP)],
+                q_ss, q_rs, NC * z + chip(-1) + k,
+            ).start()
+
+    def ring(dz):
+        return lax.rem(z + NZ + dz, NZ)
 
     def norm_passage(p, _):
         x = p_raw[p].astype(f32)
@@ -242,12 +271,19 @@
 
     relay(1)
     tblm_copy.wait()
-    deliver(q_low, z)
+    deliver(q_low, z, 0)
     relay(2)
-    deliver_both(1)
+    deliver(plus[1], ring(-1), 1)
+    deliver(minus[1], ring(1), 2)
+    forward_via(0, z)
     relay(3)
-    deliver_both(2)
-    deliver_both(3)
+    deliver(plus[2], ring(-2), 3)
+    forward_via(1, ring(-1))
+    forward_via(2, ring(1))
+    deliver(minus[2], ring(2))
+    deliver(plus[3], ring(-3))
+    forward_via(3, ring(-2))
+    deliver(minus[3], ring(3))
     p_copy.wait()
     lax.fori_loop(0, NPASS // 2, norm_passage, 0, unroll=2)
     for k in range(PIECES):
@@ -387,18 +423,40 @@
             acc = acc + wt[pos & (TILE - 1), pos >> 3] * a_ref[pos]
         return acc.astype(bf16)
 
-    def send_ret(d, _):
-        peer = lax.rem(me + d, NP)
+    def fill_ret(peer):
         for k in range(CAP):
             ret_send[CAP * peer + k] = group_grad(CAP * peer + k)
+        return ret_send.at[pl.ds(CAP * peer, CAP)]
+
+    split = NC // 2
+    for e in range(split):
         to_pool(
-            ret_send.at[pl.ds(CAP * peer, CAP)], ret_recv.at[pl.ds(CAP * me, CAP)], r_ss, r_rs, peer
+            fill_ret(NC * ring(4) + lax.rem(c + split + e, NC)),
+            ret_via.at[pl.ds(CAP * e, CAP)], r_ss, ret_vr, along_z(-2),
         ).start()
+    mine = ret_recv.at[pl.ds(CAP * me, CAP)]
+    for e in range(split):
+        peer = NC * ring(4) + lax.rem(c + e, NC)
+        to_pool(fill_ret(peer), mine, r_ss, r_rs, peer).start()
+
+    def send_ret(i, _):
+        j = i // NC
+        dz = (NZ // 2 - 1 - j // 2) * (1 - 2 * (j % 2))
+        peer = NC * ring(dz) + lax.rem(c + 1 + i % NC, NC)
+        to_pool(fill_ret(peer), mine, r_ss, r_rs, peer).start()
         return 0
 
-    lax.fori_loop(1, NP, send_ret, 0)
+    others = NP - NC - 1
+    lax.fori_loop(0, others, send_ret, 0, unroll=5)
     for k in range(CAP):
         ret_recv[CAP * me + k] = group_grad(CAP * me + k)
+    wait_bytes(ret_via, ret_vr)
+    for e in range(split):
+        to_pool(
+            ret_via.at[pl.ds(CAP * e, CAP)],
+            ret_recv.at[pl.ds(CAP * along_z(2), CAP)],
+            ret_vs, r_rs, NC * ring(-2) + lax.rem(c + split + e, NC),
+        ).start()
 
     def passage_tile(t, acc):
         qs = jnp.concatenate(
@@ -499,7 +557,8 @@
         wait_bytes(send.at[pl.ds(0, NZ - 1)], sems.at[0])
         wait_bytes(send.at[pl.ds(0, NC - 1)], sems.at[2])
     wait_bytes(q_send.at[pl.ds(0, NQ * (NZ - 1))], hop_s)
-    wait_bytes(q_send.at[pl.ds(0, CAP * NZ * (NC - 1))], q_ss)
+    wait_bytes(q_send, q_ss)
+    wait_bytes(ret_via, ret_vs)
     wait_bytes(ret_send.at[pl.ds(0, CAP * (NP - 1))], r_ss)
     wait_bytes(rs_send.at[pl.ds(0, NR - 1)], x_ss)
 
@@ -567,6 +626,8 @@
         ]
         + [pltpu.VMEM((NPASS // 2, SHARE, DIM), bf16)] * 4
         + [
+            pltpu.VMEM((4, 2 * CAP, QT, DIM), bf16),
+            pltpu.VMEM((CAP * NC // 2, QT, DIM), bf16),
             pltpu.VMEM((8, 128), i32),
             pltpu.VMEM((8, 128), i32),
             pltpu.VMEM((40, 128), i32),
@@ -579,7 +640,7 @@
         + [dma(()), dma(()), dma(()), dma((PIECES * NZ // 2,)), dma((PIECES * NZ // 2,)), dma(()), dma(())]
         + [dma((4,))] * 3
         + [dma(())] * 4
-        + [dma((2,))],
+        + [dma((2,)), dma((4,)), dma(()), dma(())],
         compiler_params=pltpu.CompilerParams(
             collective_id=0, has_side_effects=True, vmem_limit_bytes=62 * 1024 * 1024
         ),

time: 93.5 us -> 100 us (1.070)
  Pallas kernels: 92.7 us -> 99.3 us
    pallas_call x1, Pallas kernels: 87.7 us -> 94.3 us  [per_device(): pl.pallas_call(kernel, out_shape=outs, in_specs=[vmem, anywhere, vmem, vm...]
where the time goes in v5:
time: 100 us; the launch traced here: 99.9 us
  Pallas kernels  99.3 us (99%)
    pallas_call x1, Pallas kernels, per_device(): pl.pallas_call(kernel, out_shape=outs, in_specs=[vmem, anywhere, vmem, vm...  94.3 us
    pallas_call x1, Pallas kernels, per_device(): pl.pallas_call(finish, grid=(NPASS // RS_CHUNK,), out_shape=outs, in_spec...  5.03 us

profile of v5, /device:TPU:1, one launch (start us, length us, event | category | flops | bytes accessed | tf_op | source)
XLA Modules:
  0.0 99.9 jit_solution(11132424278227808603)
XLA Ops:
  0.6 94.3 %shard_map.76 = (f32[1,16]{1,0:T(1,128)}, f32[16,32,128]{2,1,0:T(8,128)}, f32[32,64,128]{2,1,0:T(8,128)}) custom-call(bf16[16,32,128]{2,1,0:T(8,128)(2,1)} %q_ref.3, bf16[32,256,128]{2,1,0:T(8,128)(2,1)} %p_any.3, s32[4,16]{1,0:T(4,128)} %bitcast.6, s32[16,16]{1,0:T(8,128)} %bitcast.5, s32[16,16]{1,0:T(8,128)} %mask_ref.1), custom_call_target="tpu_custom_call" | custom-call | tf_op jit(solution)/shard_map/pallas_call | solution.py:601
  94.9 5.0 %shard_map.77 = (f32[1,16]{1,0:T(1,128)}, f32[16,32,128]{2,1,0:T(8,128)}, f32[32,64,128]{2,1,0:T(8,128)}) custom-call(f32[1,16]{1,0:T(1,128)} %get-tuple-element.9.loss_in, bf16[16,32,128]{2,1,0:T(8,128)(2,1)} %q_ref.3, f32[16,32,128]{2,1,0:T(8,128)} %get-tuple-element.10.uq_ref, bf16[32,256,128]{2,1,0:T(8,128)(2,1)} %p_any.3, ...), custom_call_target="tpu_custom_call" | custom-call | tf_op jit(solution)/shard_map/pallas_call | solution.py:656

commit v6 on v4

--- a/solution.py
+++ b/solution.py
@@ -28,6 +28,8 @@
 GROUPS = 4
 WIDTH = 4
 SLOTS = NP * CAP
+QUERY, GROUP_SLOTS = WIDTH, WIDTH + 1
+FLAGS, FIRST = GROUP_SLOTS + GROUPS, GROUP_SLOTS + GROUPS + WIDTH
 TILE = 8
 NTILES = (SLOTS * WIDTH + NPASS * (TILE - 1)) // TILE
 SHARE = PT // NR
@@ -72,10 +74,10 @@
     q_ref, p_any, own_ref, loc_ref, mask_ref,
     loss_ref, uq_ref, up_ref,
     p_raw, p_low, q_low, plus1, plus2, plus3, minus1, minus2, minus3, far, q_send, q_recv,
-    m_a, m_b, m_c, s_a, s_b, s_c, w_a, w_b, w_c,
+    m_a, m_b, m_c, s_a, s_b, s_c,
     rows_ref, rhs_ref, soft_ref, a_ref, qn_ref, ret_send, ret_recv, rs_send, rs_recv, via_plus, via_minus, sum_plus, sum_minus,
     tbla_v, tblm_v, tblb_v, wt_v, tbla, tblm, tblb, wt,
-    sem_p, sem_tbl, hop_s, plus_r, minus_r, q_ss, q_rs, m_sem, s_sem, w_sem, r_ss, r_rs, x_ss, x_rs, v_rs,
+    sem_p, sem_tbl, hop_s, plus_r, minus_r, q_ss, q_rs, m_sem, s_sem, r_ss, r_rs, x_ss, x_rs, v_rs,
 ):
     me = lax.axis_index("pool")
     rep = lax.axis_index("rep")
@@ -153,10 +155,11 @@
     mask_f = mask_ref[...].astype(f32)
     src_r, dst_c = iota((NQ, 128), 0), iota((NQ, 128), 1)
     places = [hot((src_r == WIDTH * g + dst_c) & (dst_c < WIDTH)) for g in range(GROUPS)]
+    shifted = [
+        hot((src_r == WIDTH * g + dst_c - FLAGS) & (dst_c >= FLAGS) & (dst_c < FLAGS + WIDTH))
+        for g in range(GROUPS)
+    ]
     loc_w = jnp.concatenate([dot(loc_f, place) for place in places], axis=0)
-    mask_w = [dot(mask_f, place) for place in places]
-    pair_q = (iota((npair, 128), 0) % NQ).astype(f32)
-    loc_w = jnp.where(iota((npair, 128), 1) == WIDTH, pair_q, loc_w)
     ra, ca = iota((npair, npair), 0), iota((npair, npair), 1)
     own_row = jnp.sum(jnp.where(ra == ca, own_col, 0.0), axis=0, keepdims=True)
     same = own_col == own_row
@@ -173,7 +176,16 @@
     tbla_v[...] = index(jnp.broadcast_to(slot_wide, (8, 128)), SLOTS)
     tbla_copy = pltpu.make_async_copy(tbla_v, tbla, sem_tbl)
     tbla_copy.start()
-    put_rows(m_a, dot(s_hot, loc_w))
+    lane_q = iota((NQ, 128), 1)
+    group_slots = jnp.zeros((NQ, 128), f32)
+    for g in range(GROUPS):
+        group_slots = jnp.where(lane_q == GROUP_SLOTS + g, slot_col[NQ * g : NQ * (g + 1)], group_slots)
+    flags = [dot(mask_f, place) for place in shifted]
+    flags[0] = jnp.where((lane_q == FLAGS) | (lane_q == FIRST), 1.0, flags[0])
+    lane_n = iota((npair, 128), 1)
+    pair_rows = loc_w + jnp.concatenate([group_slots + f for f in flags], axis=0)
+    pair_rows = jnp.where(lane_n == QUERY, (iota((npair, 128), 0) % NQ).astype(f32), pair_rows)
+    put_rows(m_a, dot(s_hot, pair_rows))
     tbla_copy.wait()
     pl.semaphore_wait(barrier, NZ - 1 + NC - 1 + NR - 1)
 
@@ -209,7 +221,7 @@
     take_rows(m_b)
     r_i, c_i = iota((128, 128), 0), iota((128, 128), 1)
     picked = jnp.sum(
-        jnp.where(r_i == c_i, rows_ref[:, WIDTH : WIDTH + 1], 0.0), axis=0, keepdims=True
+        jnp.where(r_i == c_i, rows_ref[:, QUERY : QUERY + 1], 0.0), axis=0, keepdims=True
     )
     tblm_v[...] = index(jnp.broadcast_to(picked, (8, 128)), NQ)
     tblm_copy = pltpu.make_async_copy(tblm_v, tblm, sem_tbl)
@@ -277,6 +289,9 @@
     tile_r = dot_nt(fold_row, x_tile)
     rest_r = dot_nt(fold_row, x_rest)
     loc_rows = dot_nt(hot(iota((8, 128), 0) == iota((8, 128), 1)), loc_r)
+    slot_rows = dot_nt(hot(iota((8, 128), 0) + GROUP_SLOTS == iota((8, 128), 1)), loc_r)
+    valid_c = dot(loc_r, hot((r_i == c_i + FLAGS) & (c_i < WIDTH)))
+    first_row = dot_nt(hot(iota((8, 128), 1) == FIRST), loc_r)[0:1, :]
     sub8 = iota((8, 128), 0).astype(f32)
     slot_ids = iota((8, 128), 1).astype(f32)
     table = jnp.zeros((16, 128), f32)
@@ -340,37 +355,39 @@
             jnp.where(rest_c[:, j : j + 1] == lane_r, picked, 0.0), axis=1, keepdims=True
         )
         sc = jnp.where(lane_s == j, col, sc)
-    put_rows(s_a, sc)
-    first_hop(s_a, s_b, s_sem)
-    second_hop(s_b, s_c, s_sem)
-    arrived(s_c, s_sem)
-    take_rows(s_c)
-
-    own_scores = hdot(st, rows_ref[...])
-    lane_q = iota((NQ, 128), 1)
-    denom = jnp.zeros((NQ, 1), f32)
-    exps = []
+    exps = jnp.exp(sc) * valid_c
+    diag = r_i == c_i
+    part = jnp.sum(exps, axis=1, keepdims=True)
+    s_a[0:1, :] = jnp.sum(jnp.where(diag, part, 0.0), axis=0, keepdims=True)
+    s_a[1:2, :] = jnp.sum(jnp.where(diag, sc[:, 0:1], 0.0), axis=0, keepdims=True)
+    for e in range(1, NZ):
+        to_pool(s_a, s_b.at[z], s_sem.at[0], s_sem.at[1], along_z(e)).start()
+    s_b[z] = s_a[...]
+    exp_rows = hdot_nt(hot(iota((8, 128), 0) == iota((8, 128), 1)), exps)
+    wait_bytes(s_b.at[pl.ds(0, NZ - 1)], s_sem.at[1])
+    for e in range(1, NC):
+        to_pool(s_b, s_c.at[c], s_sem.at[2], s_sem.at[3], in_plane(e)).start()
+    s_c[c] = s_b[...]
+    wait_bytes(s_c.at[pl.ds(0, NC - 1)], s_sem.at[3])
+    for peer in range(NP):
+        rows_ref[CAP * peer : CAP * (peer + 1), :] = s_c[peer % NC, peer // NC]
+
+    sums = rows_ref[...]
+    twin = jnp.where(c_i % 2 == 0, pltpu.roll(sums, 127, 1), pltpu.roll(sums, 1, 1))
+    denom = jnp.zeros((1, 128), f32)
+    odd_lane = (iota((1, 128), 1) % 2).astype(f32)
     for g in range(GROUPS):
-        valid = mask_w[g]
-        if g == 0:
-            valid = jnp.where(lane_q == 0, 1.0, valid)
-        e = jnp.exp(own_scores[NQ * g : NQ * (g + 1), :]) * valid
-        exps.append(e)
-        denom = denom + jnp.sum(e, axis=1, keepdims=True)
-    losses = jnp.log(denom) - own_scores[0:NQ, 0:1]
-    loss_ref[...] = jnp.sum(
-        jnp.where(iota((NQ, NQ), 0) == iota((NQ, NQ), 1), losses, 0.0), axis=0, keepdims=True
-    )
-    dscore = [LOSS_SCALE * (e / denom) for e in exps]
-    dscore[0] = dscore[0] - jnp.where(lane_q == 0, LOSS_SCALE, 0.0)
-    w_slots = hdot(s_hot, jnp.concatenate(dscore, axis=0))
-    put_rows(w_a, w_slots)
-    first_hop(w_a, w_b, w_sem)
-    second_hop(w_b, w_c, w_sem)
-    arrived(w_c, w_sem)
-    take_rows(w_c)
-
-    w_rows = hdot_nt(hot(iota((8, 128), 0) == iota((8, 128), 1)), rows_ref[...])
+        target = slot_rows[g : g + 1, :]
+        odd = target - 2.0 * jnp.floor(target * 0.5)
+        value = jnp.where(odd == odd_lane, sums, twin)
+        denom = denom + jnp.sum(
+            jnp.where(r_i.astype(f32) == target - odd, value, 0.0), axis=0, keepdims=True
+        )
+    denom = jnp.where(denom > 0.0, denom, 1.0)
+    w_rows = LOSS_SCALE * (
+        exp_rows / denom - jnp.where(iota((8, 128), 0) == 0, first_row, 0.0)
+    )
+
     w_tile = jnp.zeros((8, 128), f32)
     for j in range(WIDTH):
         lhs = jnp.where(rest_r[j : j + 1, :] == sub8, w_rows[j : j + 1, :], 0.0)
@@ -399,6 +416,28 @@
     lax.fori_loop(1, NP, send_ret, 0)
     for k in range(CAP):
         ret_recv[CAP * me + k] = group_grad(CAP * me + k)
+
+    odd = slot_col - 2.0 * jnp.floor(slot_col * 0.5)
+    own_rows = [
+        jnp.sum(
+            jnp.where(
+                diag,
+                jnp.sum(jnp.where(c_i == CAP * me + k, sums, 0.0), axis=1, keepdims=True),
+                0.0,
+            ),
+            axis=0, keepdims=True,
+        )
+        for k in range(CAP)
+    ]
+    own = jnp.where(odd == 0.0, own_rows[0], own_rows[1])
+    lane_f = iota((npair, 128), 1).astype(f32)
+    pair_sum = jnp.sum(jnp.where(lane_f == slot_col - odd, own, 0.0), axis=1, keepdims=True)
+    pair_score = jnp.sum(jnp.where(lane_f == slot_col - odd + 1.0, own, 0.0), axis=1, keepdims=True)
+    total_sum = pair_sum[0:NQ]
+    for g in range(1, GROUPS):
+        total_sum = total_sum + pair_sum[NQ * g : NQ * (g + 1)]
+    losses = jnp.log(total_sum) - pair_score[0:NQ]
+    loss_ref[...] = jnp.sum(jnp.where(eye, losses, 0.0), axis=0, keepdims=True)
 
     def passage_tile(t, acc):
         qs = jnp.concatenate(
@@ -495,9 +534,10 @@
 
     lax.fori_loop(0, NPASS, sum_passage, 0, unroll=4)
 
-    for send, sems in ((m_a, m_sem), (s_a, s_sem), (w_a, w_sem)):
-        wait_bytes(send.at[pl.ds(0, NZ - 1)], sems.at[0])
-        wait_bytes(send.at[pl.ds(0, NC - 1)], sems.at[2])
+    wait_bytes(m_a.at[pl.ds(0, NZ - 1)], m_sem.at[0])
+    wait_bytes(m_a.at[pl.ds(0, NC - 1)], m_sem.at[2])
+    wait_bytes(s_b.at[pl.ds(0, NZ - 1)], s_sem.at[0])
+    wait_bytes(s_c.at[pl.ds(0, NC - 1)], s_sem.at[2])
     wait_bytes(q_send.at[pl.ds(0, NQ * (NZ - 1))], hop_s)
     wait_bytes(q_send.at[pl.ds(0, CAP * NZ * (NC - 1))], q_ss)
     wait_bytes(ret_send.at[pl.ds(0, CAP * (NP - 1))], r_ss)
@@ -553,8 +593,11 @@
             pltpu.VMEM((SLOTS, QT, DIM), bf16),
             pltpu.VMEM((SLOTS, QT, DIM), bf16),
         ]
-        + [rows] * 9
+        + [rows] * 3
         + [
+            pltpu.VMEM((CAP, 128), f32),
+            pltpu.VMEM((NZ, CAP, 128), f32),
+            pltpu.VMEM((NC, NZ, CAP, 128), f32),
             pltpu.VMEM((SLOTS, 128), f32),
             pltpu.VMEM((WIDTH, 128, 128), f32),
             pltpu.VMEM((NTILES, TILE * QT, PT), bf16),
@@ -577,7 +620,7 @@
             pltpu.SMEM((8, 128), f32),
         ]
         + [dma(()), dma(()), dma(()), dma((PIECES * NZ // 2,)), dma((PIECES * NZ // 2,)), dma(()), dma(())]
-        + [dma((4,))] * 3
+        + [dma((4,))] * 2
         + [dma(())] * 4
         + [dma((2,))],
         compiler_params=pltpu.CompilerParams(

time: 93.5 us -> 84.1 us (0.90)
  Pallas kernels: 92.7 us -> 83.2 us
    pallas_call x1, Pallas kernels: 87.7 us -> 78.2 us  [per_device(): pl.pallas_call(kernel, out_shape=outs, in_specs=[vmem, anywhere, vmem, vm...]
where the time goes in v6:
time: 84.1 us; the launch traced here: 83.9 us
  Pallas kernels  83.2 us (99%)
    pallas_call x1, Pallas kernels, per_device(): pl.pallas_call(kernel, out_shape=outs, in_specs=[vmem, anywhere, vmem, vm...  78.2 us
    pallas_call x1, Pallas kernels, per_device(): pl.pallas_call(finish, grid=(NPASS // RS_CHUNK,), out_shape=outs, in_spec...  5.03 us

profile of v6, /device:TPU:1, one launch (start us, length us, event | category | flops | bytes accessed | tf_op | source)
XLA Modules:
  0.0 83.9 jit_solution(14405685155580466597)
XLA Ops:
  0.6 78.2 %shard_map.76 = (f32[1,16]{1,0:T(1,128)}, f32[16,32,128]{2,1,0:T(8,128)}, f32[32,64,128]{2,1,0:T(8,128)}) custom-call(bf16[16,32,128]{2,1,0:T(8,128)(2,1)} %q_ref.3, bf16[32,256,128]{2,1,0:T(8,128)(2,1)} %p_any.3, s32[4,16]{1,0:T(4,128)} %bitcast.6, s32[16,16]{1,0:T(8,128)} %bitcast.5, s32[16,16]{1,0:T(8,128)} %mask_ref.1), custom_call_target="tpu_custom_call" | custom-call | tf_op jit(solution)/shard_map/pallas_call | solution.py:582
  78.8 5.0 %shard_map.77 = (f32[1,16]{1,0:T(1,128)}, f32[16,32,128]{2,1,0:T(8,128)}, f32[32,64,128]{2,1,0:T(8,128)}) custom-call(f32[1,16]{1,0:T(1,128)} %get-tuple-element.9.loss_in, bf16[16,32,128]{2,1,0:T(8,128)(2,1)} %q_ref.3, f32[16,32,128]{2,1,0:T(8,128)} %get-tuple-element.10.uq_ref, bf16[32,256,128]{2,1,0:T(8,128)(2,1)} %p_any.3, ...), custom_call_target="tpu_custom_call" | custom-call | tf_op jit(solution)/shard_map/pallas_call | solution.py:638

commit v7 on v6

--- a/solution.py
+++ b/solution.py
@@ -255,10 +255,10 @@
     relay(1)
     tblm_copy.wait()
     deliver(q_low, z)
+    deliver_both(1)
     relay(2)
-    deliver_both(1)
+    deliver_both(2)
     relay(3)
-    deliver_both(2)
     deliver_both(3)
     p_copy.wait()
     lax.fori_loop(0, NPASS // 2, norm_passage, 0, unroll=2)

time: 84.1 us -> 83.3 us (level)
  no operation moved by 1% of the time
where the time goes in v7:
time: 83.3 us; the launch traced here: 83.1 us
  Pallas kernels  82.4 us (99%)
    pallas_call x1, Pallas kernels, per_device(): pl.pallas_call(kernel, out_shape=outs, in_specs=[vmem, anywhere, vmem, vm...  77.4 us
    pallas_call x1, Pallas kernels, per_device(): pl.pallas_call(finish, grid=(NPASS // RS_CHUNK,), out_shape=outs, in_spec...  5.03 us

profile of v7, /device:TPU:1, one launch (start us, length us, event | category | flops | bytes accessed | tf_op | source)
XLA Modules:
  0.0 83.1 jit_solution(12489164171483295692)
XLA Ops:
  0.6 77.4 %shard_map.76 = (f32[1,16]{1,0:T(1,128)}, f32[16,32,128]{2,1,0:T(8,128)}, f32[32,64,128]{2,1,0:T(8,128)}) custom-call(bf16[16,32,128]{2,1,0:T(8,128)(2,1)} %q_ref.3, bf16[32,256,128]{2,1,0:T(8,128)(2,1)} %p_any.3, s32[4,16]{1,0:T(4,128)} %bitcast.6, s32[16,16]{1,0:T(8,128)} %bitcast.5, s32[16,16]{1,0:T(8,128)} %mask_ref.1), custom_call_target="tpu_custom_call" | custom-call | tf_op jit(solution)/shard_map/pallas_call | solution.py:582
  78.0 5.0 %shard_map.77 = (f32[1,16]{1,0:T(1,128)}, f32[16,32,128]{2,1,0:T(8,128)}, f32[32,64,128]{2,1,0:T(8,128)}) custom-call(f32[1,16]{1,0:T(1,128)} %get-tuple-element.9.loss_in, bf16[16,32,128]{2,1,0:T(8,128)(2,1)} %q_ref.3, f32[16,32,128]{2,1,0:T(8,128)} %get-tuple-element.10.uq_ref, bf16[32,256,128]{2,1,0:T(8,128)(2,1)} %p_any.3, ...), custom_call_target="tpu_custom_call" | custom-call | tf_op jit(solution)/shard_map/pallas_call | solution.py:638
